TPU v7x, 256 devices: a whole 4x4x8 slice. The times are simulated.
256 devices in a mesh: face: 8 (over y, x_lo), tile: 32 (over x_hi, z, core).
Axes of the slice: x: 4 (x_hi: 2, x_lo: 2; x = x_hi * 2 + x_lo), y: 4, z: 8, core: 2. Of those that a mesh axis runs over, the one named last changes fastest.
Arguments:
- fields: bfloat16 [8, 256, 128, 256], P('face', 'tile'), may hold values from -6 to 6
- cotangent: bfloat16 [8, 256, 128, 256], P('face', 'tile'), may hold values from -6 to 6
- edge_match: int32 [8, 2, 3], replicated, may hold values from 0 to 7, as said below
- depth_kernel: bfloat16 [7, 7, 256], replicated, may hold values from -0.875 to 0.875
- depth_bias: float32 [256], replicated, may hold values from -3 to 3
- norm_gain: float32 [256], replicated, may hold values from 0.5 to 1.5
- norm_bias: float32 [256], replicated, may hold values from -3 to 3
- expand_weight: bfloat16 [256, 1024], replicated, may hold values from -0.375 to 0.375
- expand_bias: float32 [1024], replicated, may hold values from -3 to 3
- reduce_weight: bfloat16 [1024, 256], replicated, may hold values from -0.1875 to 0.1875
- reduce_bias: float32 [256], replicated, may hold values from -3 to 3
- layer_scale: float32 [256], replicated, may hold values from 0.5 to 1.5
Outputs:
- result: bfloat16 [8, 256, 128, 256], P('face', 'tile')
- grad_fields: bfloat16 [8, 256, 128, 256], P('face', 'tile')
- grad_kernel: float32 [7, 7, 256], replicated
- grad_expand: float32 [256, 1024], replicated
- grad_reduce: float32 [1024, 256], replicated
- grad_expand_bias: float32 [1024], replicated
- grad_vectors: float32 [5, 256], replicated
Inputs may be any that keep to these rules, and one draw needn't show every extreme that they name: edge_match[f, s] = (g, s2, r): side s of strip f is glued to side s2 of strip g, rows reversed where r is 1; the gluing is symmetric; one side of strip f is glued to strip f XOR 1, the other to strip (f + 4) mod 8; at least one glued pair has reversed rows and at least one has not.
All inputs are finite; a program needn't handle non-finite values.
Results may differ from a plain program's by a relative error of at most 0.0067.
Values may be sent and summed in bfloat16 or wider, within the bound.
A program may use at most 64 MiB of HBM per device.

v0:
```python
import math

import jax
import jax.numpy as jnp
from jax import lax
from jax.sharding import PartitionSpec as P

EPSILON = 1e-06
ROOT_COEF = 0.7978845608028654
CUBIC_COEF = 0.044715


def swapped(x, axis, stride):
    return lax.ppermute(x, axis, [(i, i ^ 1 << stride) for i in range(lax.axis_size(axis))])


def padded_2(cells, sides, width):
    for axis, dim in sides:
        count = lax.axis_size(axis)
        ends = count - 1
        head = lax.slice_in_dim(cells, 0, width, axis=dim)
        tail = lax.slice_in_dim(cells, cells.shape[dim] - width, cells.shape[dim], axis=dim)
        cells = jnp.concatenate(
            [
                lax.ppermute(tail, axis, [(i, (i + 1) % count) for i in range(ends)]),
                cells,
                lax.ppermute(head, axis, [((i + 1) % count, i) for i in range(ends)]),
            ],
            axis=dim,
        )
    return cells


def gelu_pair(preact):
    argument = ROOT_COEF * (preact + CUBIC_COEF * preact * preact * preact)
    tanhed = jnp.tanh(argument)
    gelu_value = 0.5 * preact * (1.0 + tanhed)
    gelu_slope = 0.5 * (1.0 + tanhed) + 0.5 * preact * (1.0 - tanhed * tanhed) * ROOT_COEF * (
        1.0 + 3.0 * CUBIC_COEF * preact * preact
    )
    return (gelu_value, gelu_slope)


def contract_rows(left_side, right_side):
    return lax.dot_general(
        left_side, right_side, (((0,), (0,)), ((), ())), preferred_element_type=jnp.float32
    )


def contract_cols(left_side, right_side):
    return lax.dot_general(
        left_side, right_side, (((1,), (1,)), ((), ())), preferred_element_type=jnp.float32
    )


def block_pass(
    padded,
    face_grid,
    face_cot,
    kernel,
    depth_bias,
    norm_gain,
    norm_bias,
    expand_weight,
    expand_bias,
    reduce_weight,
    reduce_bias,
    layer_scale,
):
    row_count, col_count, channels = face_grid.shape
    kernel_size = kernel.shape[0]
    convolved = jnp.zeros((row_count, col_count, channels), jnp.float32) + depth_bias
    for row_off in range(kernel_size):
        for col_off in range(kernel_size):
            convolved = (
                convolved
                + kernel[row_off, col_off]
                * padded[row_off : row_off + row_count, col_off : col_off + col_count]
            )
    average = jnp.mean(convolved, axis=-1, keepdims=True)
    centred = convolved - average
    inverse = lax.rsqrt(jnp.mean(centred * centred, axis=-1, keepdims=True) + EPSILON)
    standard = centred * inverse
    normed = (
        (standard * norm_gain + norm_bias)
        .astype(jnp.bfloat16)
        .reshape(row_count * col_count, channels)
    )
    preact = jnp.dot(normed, expand_weight, preferred_element_type=jnp.float32) + expand_bias
    gelu_value, gelu_slope = gelu_pair(preact)
    activated = gelu_value.astype(jnp.bfloat16)
    branch = jnp.dot(activated, reduce_weight, preferred_element_type=jnp.float32) + reduce_bias
    residual = face_grid.reshape(row_count * col_count, channels).astype(jnp.float32)
    result = (
        (residual + layer_scale * branch)
        .astype(jnp.bfloat16)
        .reshape(row_count, col_count, channels)
    )
    upstream = face_cot.reshape(row_count * col_count, channels).astype(jnp.float32)
    grad_branch = (upstream * layer_scale).astype(jnp.bfloat16)
    grad_pre = (contract_cols(grad_branch, reduce_weight) * gelu_slope).astype(jnp.bfloat16)
    grad_normed = contract_cols(grad_pre, expand_weight).reshape(row_count, col_count, channels)
    scaled = grad_normed * norm_gain
    grad_conv = (
        scaled
        - jnp.mean(scaled, axis=-1, keepdims=True)
        - standard * jnp.mean(scaled * standard, axis=-1, keepdims=True)
    ) * inverse
    dz_padded = jnp.pad(grad_conv, ((6, 6), (6, 6), (0, 0)))
    grad_padded = jnp.zeros((row_count + 6, col_count + 6, channels), jnp.float32)
    kernel_terms = []
    for row_off in range(kernel_size):
        for col_off in range(kernel_size):
            grad_padded = (
                grad_padded
                + kernel[row_off, col_off]
                * dz_padded[
                    6 - row_off : 12 - row_off + row_count, 6 - col_off : 12 - col_off + col_count
                ]
            )
            kernel_terms.append(
                jnp.sum(
                    grad_conv
                    * padded[row_off : row_off + row_count, col_off : col_off + col_count],
                    axis=(0, 1),
                )
            )
    grad_kernel = jnp.stack(kernel_terms).reshape(kernel_size, kernel_size, channels)
    grad_expand = contract_rows(normed, grad_pre)
    grad_reduce = contract_rows(activated, grad_branch)
    grad_expand_bias = jnp.sum(grad_pre.astype(jnp.float32), axis=0)
    vectors = jnp.stack(
        [
            jnp.sum(grad_conv, axis=(0, 1)),
            jnp.sum(grad_normed * standard, axis=(0, 1)),
            jnp.sum(grad_normed, axis=(0, 1)),
            jnp.sum(upstream, axis=0) * layer_scale,
            jnp.sum(upstream * branch, axis=0),
        ]
    )
    return (result, grad_padded, (grad_kernel, grad_expand, grad_reduce, grad_expand_bias, vectors))


def mirrored(strips, backward):
    tile_count = lax.axis_size("tile")
    carried = strips
    for bit_index in range(tile_count.bit_length() - 1):
        if backward:
            carried = swapped(carried.astype(jnp.bfloat16), "tile", bit_index).astype(carried.dtype)
        else:
            carried = swapped(carried, "tile", bit_index)
    return carried


def partner_strips(strips, edge_match, backward):
    flipped = mirrored(strips, backward)
    both_kinds = jnp.stack([strips, flipped])
    own_index = lax.axis_index("face")
    own_match = lax.dynamic_index_in_dim(edge_match, own_index, 0, keepdims=False)
    received = []
    if backward:
        gathered = lax.all_gather(
            both_kinds[None].astype(jnp.bfloat16), "face", axis=0, tiled=True
        ).astype(jnp.float32)
    else:
        gathered = lax.all_gather(both_kinds[None], "face", axis=0, tiled=True)
    stacked_all = gathered.reshape((-1,) + gathered.shape[3:])
    for edge_side in range(2):
        partner = own_match[edge_side, 0]
        other_side = own_match[edge_side, 1]
        reverse_flag = own_match[edge_side, 2]
        picked_strip = lax.dynamic_index_in_dim(
            stacked_all, (partner * 2 + reverse_flag) * 2 + other_side, 0, keepdims=False
        )
        received.append(jnp.where(reverse_flag == 1, jnp.flip(picked_strip, 0), picked_strip))
    return received


def widen(tile_band, edge_match):
    col_count = tile_band.shape[1]
    strips = jnp.stack([tile_band[:, 0:3], jnp.flip(tile_band[:, col_count - 3 :], 1)])
    west_side, east_side = partner_strips(strips, edge_match, False)
    widened = jnp.concatenate([jnp.flip(west_side, 1), tile_band, east_side], axis=1)
    return padded_2(widened, (("tile", 0),), 3)


def fold_back(grad_padded, edge_match):
    row_count = grad_padded.shape[0] - 6
    col_count = grad_padded.shape[1] - 6
    rim_rows = jnp.concatenate([grad_padded[0:3], grad_padded[row_count + 3 :]], axis=0)
    arrived = padded_2(rim_rows.astype(jnp.bfloat16), (("tile", 0),), 3).astype(rim_rows.dtype)
    middle = grad_padded[3 : row_count + 3]
    middle = middle.at[0:3].add(arrived[0:3])
    middle = middle.at[row_count - 3 :].add(arrived[9:12])
    west_ghost = jnp.flip(middle[:, 0:3], 1)
    east_ghost = middle[:, col_count + 3 :]
    west_back, east_back = partner_strips(jnp.stack([west_ghost, east_ghost]), edge_match, True)
    interior = middle[:, 3 : col_count + 3]
    interior = interior.at[:, 0:3].add(west_back)
    interior = interior.at[:, col_count - 3 :].add(jnp.flip(east_back, 1))
    return interior


def shards(
    fields,
    cotangent,
    edge_match,
    depth_kernel,
    depth_bias,
    norm_gain,
    norm_bias,
    expand_weight,
    expand_bias,
    reduce_weight,
    reduce_bias,
    layer_scale,
):
    tile_band = fields[0]
    row_count, col_count, channels = tile_band.shape
    padded = widen(tile_band, edge_match).astype(jnp.float32)
    result, grad_padded, terms = block_pass(
        padded,
        tile_band,
        cotangent[0],
        depth_kernel.astype(jnp.float32),
        depth_bias,
        norm_gain,
        norm_bias,
        expand_weight,
        expand_bias,
        reduce_weight,
        reduce_bias,
        layer_scale,
    )
    interior = fold_back(grad_padded, edge_match)
    grad_fields = (cotangent[0].astype(jnp.float32) + interior).astype(jnp.bfloat16)
    grad_kernel, grad_expand, grad_reduce, grad_expand_bias, vectors = terms
    grad_kernel, grad_expand, grad_reduce, grad_expand_bias, vectors = lax.psum(
        (grad_kernel, grad_expand, grad_reduce, grad_expand_bias, vectors), ("face", "tile")
    )
    cell_total = lax.axis_size("face") * lax.axis_size("tile") * row_count * col_count
    factor = 1.0 / math.sqrt(cell_total)
    return (
        result[None],
        grad_fields[None],
        grad_kernel * factor,
        grad_expand * factor,
        grad_reduce * factor,
        grad_expand_bias * factor,
        vectors * factor,
    )


def solution(mesh):
    return jax.shard_map(
        shards,
        mesh=mesh,
        in_specs=(
            P("face", "tile", None, None),
            P("face", "tile", None, None),
            P(),
            P(),
            P(),
            P(),
            P(),
            P(),
            P(),
            P(),
            P(),
            P(),
        ),
        out_specs=(
            P("face", "tile", None, None),
            P("face", "tile", None, None),
            P(),
            P(),
            P(),
            P(),
            P(),
        ),
        check_vma=False,
    )
```

profile of v0, /device:TPU:1, one launch (start us, length us, event | category | flops | bytes accessed | tf_op | source)
XLA Modules:
  0.0 504.6 jit_solution(17378685577433569779)
XLA Ops:
  8.3 3.3 collective-permute-start
  19.8 5.2 %collective-permute-start.3 = (bf16[2,8,3,256]{3,2,1,0:T(4,128)(2,1)S(1)}, bf16[2,8,3,256]{3,2,1,0:T(4,128)(2,1)S(1)}, u32[]{:S(2)}, u32[]{:S(2)}) collective-permute-start(bf16[2,8,3,256]{3,2,1,0:T(4,128)(2,1)S(1)} %collective-permute-done.2), channel_id=1, source_target_pairs={{0,8},{1,9},{2,10},{3,11},{4,12},{5,13},{6,14},{7,15},{8,0},{9,1},... | collective-permute-start | bytes 73736 | tf_op jit(solution)/shard_map/ppermute | solution.py:14
  26.5 2.5 collective-permute-start.4
  36.1 23.9 %all-gather = bf16[16,2,8,3,256]{4,2,3,1,0:T(8,128)(2,1)S(1)} all-gather(bf16[2,2,8,3,256]{4,2,3,1,0:T(8,128)(2,1)S(1)} %copy.28), channel_id=2, replica_groups=mesh['face'=8,'tile'=32] {'face'}, dimensions={0}, use_global_device_ids=true | all-gather | bytes 442368 | tf_op jit(solution)/shard_map/all_gather | solution.py:166
  60.4 12.0 %collective-permute-start.5 = (bf16[3,134,256]{2,1,0:T(8,128)(2,1)S(1)}, bf16[3,134,256]{2,1,0:T(8,128)(2,1)S(1)}, u32[]{:S(2)}, u32[]{:S(2)}) collective-permute-start(bf16[3,134,256]{2,1,0:T(8,128)(2,1)S(1)} %get-tuple-element.134), channel_id=1, source_target_pairs={{0,1},{1,2},{2,3},{3,4},{4,5},{5,6},{6,7},{7,8},{8,9},{9,10},{10,1... | collective-permute-start | bytes 617480 | tf_op jit(solution)/shard_map/ppermute | solution.py:25
  72.4 2.1 collective-permute-start.6
  76.1 3.4 collective-permute-done.6
  79.7 9.2 %fusion.117 = (f32[8,128]{1,0:T(8,128)S(1)}, f32[8,128,256]{2,1,0:T(8,128)S(1)}) fusion(f32[14,134,256]{2,1,0:T(8,128)S(1)} %maximum_convert_fusion, f32[256]{0:T(256)} %bitcast.286, f32[256]{0:T(256)} %bitcast.284, f32[256]{0:T(256)} %bitcast.282, f32[256]{0:T(256)} %bitcast.280, f32[256]{0:T(256)} %bitcast.278, f32[256]{0:T(256)} %bitcast.276, ...), kind=kLoop, calls=%fused_computation.271 | loop fusion | flops 25951232 | bytes 52484096 | tf_op jit(solution)/shard_map/reduce_sum | solution.py:80
  92.4 2.2 fusion.108
  94.6 3.8 convert_reduce_fusion
  100.7 3.6 multiply_reduce_fusion.1
  106.5 2.4 multiply_reduce_fusion.19
  109.3 17.3 %fusion.115 = (bf16[14,134,256]{2,1,0:T(8,128)(2,1)S(1)}, f32[14,134,256]{2,1,0:T(8,128)S(1)}) fusion(f32[256]{0:T(256)} %bitcast.287, f32[256]{0:T(256)} %bitcast.285, f32[256]{0:T(256)} %bitcast.283, f32[256]{0:T(256)S(1)} %bitcast.281, f32[256]{0:T(256)S(1)} %bitcast.279, f32[256]{0:T(256)S(1)} %bitcast.277, f32[256]{0:T(256)S(1)} %bitcast.275, ...), kind=kLoop, calls=%fused_computation.270 | loop fusion | flops 47065088 | bytes 3980288 | tf_op jit(solution)/shard_map/convert.10
  128.8 2.4 collective-permute-start.8
  133.0 3.0 collective-permute-done.8
  136.6 3.3 fusion.124
  140.3 83.3 %all-reduce.1 = (f32[7,7,256]{2,1,0:T(8,128)S(1)}, f32[1024]{0:T(1024)S(1)}, f32[5,256]{1,0:T(8,128)S(1)}) all-reduce(f32[7,7,256]{2,1,0:T(8,128)S(1)} %reshape.242, f32[1024]{0:T(1024)S(1)} %copy-done.68, f32[5,256]{1,0:T(8,128)S(1)} %stack.271), channel_id=1, replica_groups=mesh['face'=8,'tile'=32] {'face','tile'}, use_global_device_ids=true, to_apply=%region_53.54 | all-reduce | flops 14848 | bytes 118784 | tf_op jit(solution)/shard_map/psum | solution.py:238
  224.2 2.1 collective-permute-done.10
  227.0 3.1 collective-permute-done.11
  232.8 4.0 collective-permute-done.12
  238.1 3.0 collective-permute-done.13
  241.2 23.5 %all_gather.7 = bf16[8,2,2,8,3,256]{5,3,4,2,1,0:T(8,128)(2,1)S(1)} all-gather(bf16[1,2,2,8,3,256]{5,3,4,2,1,0:T(8,128)(2,1)S(1)} %copy.31), channel_id=1, replica_groups=mesh['face'=8,'tile'=32] {'face'}, dimensions={0}, use_global_device_ids=true | all-gather | bytes 442368 | tf_op jit(solution)/shard_map/all_gather | solution.py:162
  266.3 228.1 %all-reduce.5.cloned.1.call-done = (f32[256,1024]{1,0:T(8,128)}, f32[1024,256]{1,0:T(8,128)}) async-done(((f32[256,1024]{1,0:T(8,128)}, f32[1024,256]{1,0:T(8,128)}), (f32[256,1024]{1,0:T(8,128)}, f32[1024,256]{1,0:T(8,128)})) %all-reduce.5.cloned.1.call-update) | async-done | bytes 2097168 | tf_op jit(solution)/shard_map/psum | solution.py:238
  494.3 2.4 broadcast_multiply_fusion
  (238 shorter events, 34.8 us)
Async XLA Ops:
  7.2 83.3 %copy-start = (bf16[256,1024]{1,0:T(8,128)(2,1)S(1)}, bf16[256,1024]{1,0:T(8,128)(2,1)}, u32[]{:S(2)}) copy-start(bf16[256,1024]{1,0:T(8,128)(2,1)} %param.27) | copy-start | bytes 1572868
  7.2 53.1 %copy-start.1 = (bf16[1,8,128,256]{3,2,1,0:T(8,128)(2,1)S(1)}, bf16[1,8,128,256]{3,2,1,0:T(8,128)(2,1)}, u32[]{:S(2)}) copy-start(bf16[1,8,128,256]{3,2,1,0:T(8,128)(2,1)} %param.20) | copy-start | bytes 1572868
  7.2 487.1 %all-reduce.5.cloned.1.call-start = ((), (), s32[]{:S(2)}) async-start(), calls=%async_computation | async-start | bytes 4194304 | tf_op jit(solution)/shard_map/psum | solution.py:238
  8.3 4.9 collective-permute-start
  13.2 2.9 collective-permute-start.1
  16.1 3.7 collective-permute-start.2
  19.8 6.8 %collective-permute-start.3 = (bf16[2,8,3,256]{3,2,1,0:T(4,128)(2,1)S(1)}, bf16[2,8,3,256]{3,2,1,0:T(4,128)(2,1)S(1)}, u32[]{:S(2)}, u32[]{:S(2)}) collective-permute-start(bf16[2,8,3,256]{3,2,1,0:T(4,128)(2,1)S(1)} %collective-permute-done.2), channel_id=1, source_target_pairs={{0,8},{1,9},{2,10},{3,11},{4,12},{5,13},{6,14},{7,15},{8,0},{9,1},... | collective-permute-start | bytes 73736 | tf_op jit(solution)/shard_map/ppermute | solution.py:14
  26.5 9.5 %collective-permute-start.4 = (bf16[2,8,3,256]{3,2,1,0:T(4,128)(2,1)S(1)}, bf16[2,8,3,256]{3,2,1,0:T(4,128)(2,1)S(1)}, u32[]{:S(2)}, u32[]{:S(2)}) collective-permute-start(bf16[2,8,3,256]{3,2,1,0:T(4,128)(2,1)S(1)} %collective-permute-done.3), channel_id=1, source_target_pairs={{0,16},{1,17},{2,18},{3,19},{4,20},{5,21},{6,22},{7,23},{8,24},{9,... | collective-permute-start | bytes 73736 | tf_op jit(solution)/shard_map/ppermute | solution.py:14
  60.4 15.7 %collective-permute-start.5 = (bf16[3,134,256]{2,1,0:T(8,128)(2,1)S(1)}, bf16[3,134,256]{2,1,0:T(8,128)(2,1)S(1)}, u32[]{:S(2)}, u32[]{:S(2)}) collective-permute-start(bf16[3,134,256]{2,1,0:T(8,128)(2,1)S(1)} %get-tuple-element.134), channel_id=1, source_target_pairs={{0,1},{1,2},{2,3},{3,4},{4,5},{5,6},{6,7},{7,8},{8,9},{9,10},{10,1... | collective-permute-start | bytes 617480 | tf_op jit(solution)/shard_map/ppermute | solution.py:25
  72.4 7.1 %collective-permute-start.6 = (bf16[3,134,256]{2,1,0:T(8,128)(2,1)S(1)}, bf16[3,134,256]{2,1,0:T(8,128)(2,1)S(1)}, u32[]{:S(2)}, u32[]{:S(2)}) collective-permute-start(bf16[3,134,256]{2,1,0:T(8,128)(2,1)S(1)} %get-tuple-element.135), channel_id=1, source_target_pairs={{1,0},{2,1},{3,2},{4,3},{5,4},{6,5},{7,6},{8,7},{9,8},{10,9},{11,1... | collective-permute-start | bytes 617480 | tf_op jit(solution)/shard_map/ppermute | solution.py:27
  79.7 9.7 %copy-start.9 = (f32[256]{0:T(256)S(1)}, f32[256]{0:T(256)}, u32[]{:S(2)}) copy-start(f32[256]{0:T(256)} %param.25) | copy-start | bytes 3076
  94.6 3.8 copy-start.78
  126.6 4.6 copy-start.77
  126.6 4.6 copy-start.79
  126.7 6.2 %collective-permute-start.7 = (bf16[3,134,256]{2,1,0:T(8,128)(2,1)S(1)}, bf16[3,134,256]{2,1,0:T(8,128)(2,1)S(1)}, u32[]{:S(2)}, u32[]{:S(2)}) collective-permute-start(bf16[3,134,256]{2,1,0:T(8,128)(2,1)S(1)} %get-tuple-element.130), channel_id=1, source_target_pairs={{0,1},{1,2},{2,3},{3,4},{4,5},{5,6},{6,7},{7,8},{8,9},{9,10},{10,1... | collective-permute-start | bytes 617480 | tf_op jit(solution)/shard_map/ppermute | solution.py:25
  128.8 7.1 %collective-permute-start.8 = (bf16[3,134,256]{2,1,0:T(8,128)(2,1)S(1)}, bf16[3,134,256]{2,1,0:T(8,128)(2,1)S(1)}, u32[]{:S(2)}, u32[]{:S(2)}) collective-permute-start(bf16[3,134,256]{2,1,0:T(8,128)(2,1)S(1)} %get-tuple-element.131), channel_id=1, source_target_pairs={{1,0},{2,1},{3,2},{4,3},{5,4},{6,5},{7,6},{8,7},{9,8},{10,9},{11,1... | collective-permute-start | bytes 617480 | tf_op jit(solution)/shard_map/ppermute | solution.py:27
  136.4 3.8 copy-start.67
  136.5 3.8 copy-start.68
  136.5 87.1 %collective-permute-start.9 = (bf16[2,8,3,256]{3,2,1,0:T(4,128)(2,1)S(1)}, bf16[2,8,3,256]{3,2,1,0:T(4,128)(2,1)S(1)}, u32[]{:S(2)}, u32[]{:S(2)}) collective-permute-start(bf16[2,8,3,256]{3,2,1,0:T(4,128)(2,1)S(1)} %maximum_convert_fusion.1), channel_id=1, source_target_pairs={{0,1},{1,0},{2,3},{3,2},{4,5},{5,4},{6,7},{7,6},{8,9},{9,8},{10,11... | collective-permute-start | bytes 73736 | tf_op jit(solution)/shard_map/ppermute | solution.py:14
  223.6 2.8 collective-permute-start.10
  226.4 3.7 collective-permute-start.11
  230.1 6.7 %collective-permute-start.12 = (bf16[2,8,3,256]{3,2,1,0:T(4,128)(2,1)S(1)}, bf16[2,8,3,256]{3,2,1,0:T(4,128)(2,1)S(1)}, u32[]{:S(2)}, u32[]{:S(2)}) collective-permute-start(bf16[2,8,3,256]{3,2,1,0:T(4,128)(2,1)S(1)} %collective-permute-done.11), channel_id=1, source_target_pairs={{0,8},{1,9},{2,10},{3,11},{4,12},{5,13},{6,14},{7,15},{8,0},{9,1},... | collective-permute-start | bytes 73736 | tf_op jit(solution)/shard_map/ppermute | solution.py:14
  236.8 4.3 collective-permute-start.13
  238.0 27.3 %copy-start.7 = (bf16[1,8,128,256]{3,2,1,0:T(8,128)(2,1)S(1)}, bf16[1,8,128,256]{3,2,1,0:T(8,128)(2,1)}, u32[]{:S(2)}) copy-start(bf16[1,8,128,256]{3,2,1,0:T(8,128)(2,1)} %param.21) | copy-start | bytes 1572868
  (71 other events, 209.4 us)
Sparse Core Ops, SparseCore 0:
  232.9 261.3 all-reduce.4
where the time goes:
time: 506 us; the launch traced here: 505 us
  waiting for transfers between devices  249 us (49%)
  blocking collectives  131 us (26%)
  other arithmetic  46 us (9%)
  starting transfers between devices  34.9 us (7%)
  between operations  20.8 us (4%)
  matrix products  14.2 us (3%)
  local copies, waits for them, and re-layouts  8.93 us (2%)
    psum x1, waiting for transfers between devices, shards(): lax.psum((grad_kernel, grad_expand, grad_reduce, grad_expand_bias, vector...  228 us
    psum x1, blocking collectives, shards(): lax.psum((grad_kernel, grad_expand, grad_reduce, grad_expand_bias, vector...  83.3 us
    all_gather x1, blocking collectives, partner_strips(): gathered = lax.all_gather(both_kinds[None], 'face', axis=0, tiled=True)  23.9 us
    all_gather x1, blocking collectives, partner_strips(): lax.all_gather(both_kinds[None].astype(jnp.bfloat16), 'face', axis=0, til...  23.5 us
    another operation x2, other arithmetic  17.3 us
    ppermute x10, starting transfers between devices, swapped(): lax.ppermute(x, axis, [(i, i ^ 1 << stride) for i in range(lax.axis_size(...  16.3 us
    ppermute x10, waiting for transfers between devices, swapped(): lax.ppermute(x, axis, [(i, i ^ 1 << stride) for i in range(lax.axis_size(...  14.6 us
    ppermute x2, starting transfers between devices, padded_2(): lax.ppermute(tail, axis, [(i, (i + 1) % count) for i in range(ends)])  14.1 us
  transfers between devices with their start and end apart: 15, of which 10 were waited for; matrix products, arithmetic and copies ran while one was open for 3% of the time, Pallas kernels for 0%

commit v1 on v0

v1 whole, which is shorter than its diff:
```python
import functools
import math

import jax
import jax.numpy as jnp
from jax import lax
from jax.experimental import pallas as pl
from jax.experimental.pallas import tpu as pltpu
from jax.sharding import PartitionSpec as P

EPSILON = 1e-06
ROOT_COEF = 0.7978845608028654
CUBIC_COEF = 0.044715
MESH = pl.DeviceIdType.MESH
FACES = 8
TILES = 32
F32 = jnp.float32
BF16 = jnp.bfloat16


def halo_plan(face, tile):
    beside = face + 1 - 2 * lax.rem(face, 2)
    across = lax.rem(face + 4, FACES)
    plan = [
        ("up", (face, lax.rem(tile + TILES - 1, TILES))),
        ("down", (face, lax.rem(tile + 1, TILES))),
    ]
    for link, partner in enumerate((beside, across)):
        for flip in range(2):
            for place in range(3):
                if flip == 0:
                    target = tile + TILES + 1 - place
                else:
                    target = 2 * TILES - tile - place
                plan.append(((link, flip, place), (partner, lax.rem(target, TILES))))
    return plan


def halo_kernel(rows_ref, strips_ref, above_ref, below_ref, ghosts_ref, send_sem, recv_sem):
    plan = halo_plan(lax.axis_index("face"), lax.axis_index("tile"))
    barrier = pltpu.get_barrier_semaphore()
    for _, target in plan:
        pl.semaphore_signal(barrier, inc=1, device_id=target, device_id_type=MESH)
    pl.semaphore_wait(barrier, len(plan))
    row_count = rows_ref.shape[0]
    copies = []
    for index, (kind, target) in enumerate(plan):
        if kind == "up":
            source, landing = rows_ref.at[0:3], below_ref
        elif kind == "down":
            source, landing = rows_ref.at[row_count - 3 : row_count], above_ref
        else:
            link, flip, place = kind
            source, landing = strips_ref.at[link], ghosts_ref.at[link, flip, place]
        copy = pltpu.make_async_remote_copy(
            src_ref=source,
            dst_ref=landing,
            send_sem=send_sem.at[index],
            recv_sem=recv_sem.at[index],
            device_id=target,
            device_id_type=MESH,
        )
        copy.start()
        copies.append(copy)
    for copy in copies:
        copy.wait()


def exchange(rows, strips, collective_id):
    row_count, col_count, channels = rows.shape
    vmem = pl.BlockSpec(memory_space=pltpu.VMEM)
    return pl.pallas_call(
        halo_kernel,
        out_shape=(
            jax.ShapeDtypeStruct((3, col_count, channels), BF16),
            jax.ShapeDtypeStruct((3, col_count, channels), BF16),
            jax.ShapeDtypeStruct((2, 2, 3) + strips.shape[1:], BF16),
        ),
        in_specs=[vmem] * 2,
        out_specs=(vmem,) * 3,
        scratch_shapes=[pltpu.SemaphoreType.DMA((14,)), pltpu.SemaphoreType.DMA((14,))],
        compiler_params=pltpu.CompilerParams(collective_id=collective_id, has_side_effects=True),
    )(rows, strips)


def halo(rows, own_match):
    def at(index):
        return index

    row_count, col_count, channels = rows.shape
    face, tile = lax.axis_index("face"), lax.axis_index("tile")
    beside_side = jnp.where(own_match[0, 0] == jnp.bitwise_xor(face, 1), 0, 1)
    west = jnp.moveaxis(rows[:, 0:3], 1, 0)
    east = jnp.moveaxis(jnp.flip(rows[:, col_count - 3 :], 1), 1, 0)
    strips = jnp.where(beside_side == 0, jnp.stack([west, east]), jnp.stack([east, west]))
    return strips, beside_side


def unpack(above, below, ghosts, own_match, beside_side):
    tile = lax.axis_index("tile")
    first, last = tile == 0, tile == TILES - 1
    above = jnp.where(first, jnp.zeros_like(above), above)
    below = jnp.where(last, jnp.zeros_like(below), below)
    turned = jnp.flip(ghosts[:, 1], 3)
    ext = []
    for kind in (ghosts[:, 0], turned):
        ext.append(jnp.concatenate([kind[:, 0, :, 5:8], kind[:, 1], kind[:, 2, :, 0:3]], axis=2))
    inside = jnp.arange(14)
    inside = ((inside >= 3) | ~first) & ((inside < 11) | ~last)
    sides = []
    for side in range(2):
        link = jnp.where(beside_side == side, 0, 1)
        pair = jnp.where(own_match[side, 2] == 1, ext[1], ext[0])
        ghost = jnp.where(link == 0, pair[0], pair[1])
        ghost = jnp.where(inside[None, :, None], ghost, jnp.zeros_like(ghost))
        sides.append(jnp.moveaxis(ghost, 0, 1))
    return above, below, sides


def coordinates():
    face, tile = lax.axis_index("face"), lax.axis_index("tile")
    core = lax.rem(tile, 2)
    z = lax.rem(lax.div(tile, 2), 8)
    x = 2 * lax.div(tile, 16) + lax.rem(face, 2)
    y = lax.div(face, 2)
    return x, y, z, core


def device_at(x, y, z, core):
    return (2 * y + lax.rem(x, 2), 16 * lax.div(x, 2) + 2 * z + core)


def reduce_kernel(
    expand_ref,
    reduce_ref,
    small_ref,
    expand_out,
    reduce_out,
    small_out,
    src,
    from_core,
    sum_core,
    from_a,
    sum_a,
    from_b,
    sum_b,
    from_z,
    gathered,
    small_core,
    small_sum,
    small_x,
    small_sum_x,
    small_y,
    small_z,
    big_send,
    big_recv,
    small_send,
    small_recv,
    scale,
):
    x, y, z, core = coordinates()
    sibling = device_at(x, y, z, 1 - core)

    def x_peer(step):
        return device_at(lax.rem(x + step, 4), y, z, core)

    def y_peer(step):
        return device_at(x, lax.rem(y + step, 4), z, core)

    def z_peer(step):
        return device_at(x, y, lax.rem(z + step, 8), core)

    place_a = x + core * (y - x)
    place_b = y + core * (x - y)

    def a_peer(step):
        new = lax.rem(place_a + step, 4)
        return device_at(new + core * (x - new), y + core * (new - y), z, core)

    def b_peer(step):
        new = lax.rem(place_b + step, 4)
        return device_at(x + core * (new - x), new + core * (y - new), z, core)

    barrier = pltpu.get_barrier_semaphore()
    peers = [sibling]
    peers += [x_peer(step) for step in range(1, 4)]
    peers += [y_peer(step) for step in range(1, 4)]
    peers += [z_peer(step) for step in range(1, 8)]
    for peer in peers:
        pl.semaphore_signal(barrier, inc=1, device_id=peer, device_id_type=MESH)

    def fill_expand(row, carry):
        block = expand_ref[pl.ds(pl.multiple_of(row * 16, 16), 16), :].astype(BF16)
        for col in range(8):
            src[0, row * 8 + col] = block[:, col * 128 : col * 128 + 128]
        return carry

    def fill_reduce(row, carry):
        block = reduce_ref[pl.ds(pl.multiple_of(row * 16, 16), 16), :].astype(BF16)
        for col in range(2):
            src[1, row * 2 + col] = block[:, col * 128 : col * 128 + 128]
        return carry

    lax.fori_loop(0, 16, fill_expand, 0)
    lax.fori_loop(0, 64, fill_reduce, 0)
    pl.semaphore_wait(barrier, len(peers))

    counters = [0, 0]

    def big(source, landing, target):
        index = counters[0]
        counters[0] += 1
        copy = pltpu.make_async_remote_copy(
            source, landing, big_send.at[index], big_recv.at[index], target, MESH
        )
        copy.start()
        return copy

    def small(source, landing, target):
        index = counters[1]
        counters[1] += 1
        copy = pltpu.make_async_remote_copy(
            source, landing, small_send.at[index], small_recv.at[index], target, MESH
        )
        copy.start()
        return copy

    def finish(copies):
        for copy in copies:
            copy.wait()

    small_copies = [small(small_ref, small_core, sibling)]
    big_copies = [big(src.at[1 - core], from_core, sibling)]
    finish(small_copies)
    small_sum[...] = small_ref[...] + small_core[...]
    small_copies = []
    for step in range(1, 4):
        chunk = lax.rem(x + step, 4)
        small_copies.append(small(small_sum.at[chunk], small_x.at[step - 1], x_peer(step)))
    finish(big_copies)

    def add_core(index, carry):
        sum_core[index] = (src[core, index].astype(F32) + from_core[index].astype(F32)).astype(BF16)
        return carry

    lax.fori_loop(0, 128, add_core, 0, unroll=8)
    big_copies = []
    for step in range(1, 4):
        chunk = lax.rem(place_a + step, 4)
        big_copies.append(
            big(sum_core.at[pl.ds(chunk * 32, 32)], from_a.at[step - 1], a_peer(step))
        )
    finish(small_copies)
    small_sum_x[...] = small_sum[x] + small_x[0] + small_x[1] + small_x[2]
    small_copies = []
    for step in range(1, 4):
        chunk = lax.rem(y + step, 4)
        small_copies.append(small(small_sum_x.at[chunk], small_y.at[step - 1], y_peer(step)))
    finish(big_copies)

    def add_a(index, carry):
        total = sum_core[place_a * 32 + index].astype(F32)
        for step in range(3):
            total = total + from_a[step, index].astype(F32)
        sum_a[index] = total.astype(BF16)
        return carry

    lax.fori_loop(0, 32, add_a, 0, unroll=8)
    big_copies = []
    for step in range(1, 4):
        chunk = lax.rem(place_b + step, 4)
        big_copies.append(big(sum_a.at[pl.ds(chunk * 8, 8)], from_b.at[step - 1], b_peer(step)))
    finish(small_copies)
    small_z[z] = small_sum_x[y] + small_y[0] + small_y[1] + small_y[2]
    small_copies = []
    for step in range(1, 8):
        small_copies.append(small(small_z.at[z], small_z.at[z], z_peer(step)))
    finish(big_copies)

    def add_b(index, carry):
        total = sum_a[place_b * 8 + index].astype(F32)
        for step in range(3):
            total = total + from_b[step, index].astype(F32)
        sum_b[index] = total.astype(BF16)
        return carry

    lax.fori_loop(0, 8, add_b, 0, unroll=8)
    big_copies = []
    for step in range(1, 8):
        big_copies.append(big(sum_b.at[lax.rem(z + step, 8)], from_z.at[step - 1], z_peer(step)))
    finish(small_copies)
    total = small_z[0]
    for step in range(1, 8):
        total = total + small_z[step]
    small_out[x, y] = total * scale
    small_copies = []
    for step in range(1, 4):
        small_copies.append(small(small_out.at[x, y], small_out.at[x, y], y_peer(step)))
    finish(big_copies)
    total = sum_b[z].astype(F32)
    for step in range(7):
        total = total + from_z[step].astype(F32)
    own = place_a * 32 + place_b * 8 + z
    gathered[core, own] = total.astype(BF16)
    big_copies = []
    for step in range(1, 8):
        big_copies.append(big(gathered.at[core, own], gathered.at[core, own], z_peer(step)))
    finish(small_copies)
    small_copies = []
    for step in range(1, 4):
        small_copies.append(small(small_out.at[x], small_out.at[x], x_peer(step)))
    finish(big_copies)
    block = pl.ds(place_a * 32 + place_b * 8, 8)
    big_copies = []
    for step in range(1, 4):
        big_copies.append(big(gathered.at[core, block], gathered.at[core, block], b_peer(step)))
    finish(big_copies)
    wide = pl.ds(place_a * 32, 32)
    big_copies = []
    for step in range(1, 4):
        big_copies.append(big(gathered.at[core, wide], gathered.at[core, wide], a_peer(step)))
    finish(big_copies)
    big_copies = [big(gathered.at[core], gathered.at[core], sibling)]
    finish(small_copies)
    finish(big_copies)

    def empty_expand(row, carry):
        rows = pl.ds(pl.multiple_of(row * 16, 16), 16)
        for col in range(8):
            expand_out[rows, col * 128 : col * 128 + 128] = (
                gathered[0, row * 8 + col].astype(F32) * scale
            )
        return carry

    def empty_reduce(row, carry):
        rows = pl.ds(pl.multiple_of(row * 16, 16), 16)
        for col in range(2):
            reduce_out[rows, col * 128 : col * 128 + 128] = (
                gathered[1, row * 2 + col].astype(F32) * scale
            )
        return carry

    lax.fori_loop(0, 16, empty_expand, 0)
    lax.fori_loop(0, 64, empty_reduce, 0)


def reduce_all(grad_expand, grad_reduce, small, scale):
    vmem = pl.BlockSpec(memory_space=pltpu.VMEM)
    tile = (16, 128)
    return pl.pallas_call(
        functools.partial(reduce_kernel, scale=scale),
        out_shape=(
            jax.ShapeDtypeStruct(grad_expand.shape, F32),
            jax.ShapeDtypeStruct(grad_reduce.shape, F32),
            jax.ShapeDtypeStruct(small.shape, F32),
        ),
        in_specs=[vmem] * 3,
        out_specs=(vmem,) * 3,
        scratch_shapes=[
            pltpu.VMEM((2, 128) + tile, BF16),
            pltpu.VMEM((128,) + tile, BF16),
            pltpu.VMEM((128,) + tile, BF16),
            pltpu.VMEM((3, 32) + tile, BF16),
            pltpu.VMEM((32,) + tile, BF16),
            pltpu.VMEM((3, 8) + tile, BF16),
            pltpu.VMEM((8,) + tile, BF16),
            pltpu.VMEM((7,) + tile, BF16),
            pltpu.VMEM((2, 128) + tile, BF16),
            pltpu.VMEM((4, 4, 8, 128), F32),
            pltpu.VMEM((4, 4, 8, 128), F32),
            pltpu.VMEM((3, 4, 8, 128), F32),
            pltpu.VMEM((4, 8, 128), F32),
            pltpu.VMEM((3, 8, 128), F32),
            pltpu.VMEM((8, 8, 128), F32),
            pltpu.SemaphoreType.DMA((28,)),
            pltpu.SemaphoreType.DMA((28,)),
            pltpu.SemaphoreType.DMA((20,)),
            pltpu.SemaphoreType.DMA((20,)),
        ],
        compiler_params=pltpu.CompilerParams(collective_id=2, has_side_effects=True),
    )(grad_expand, grad_reduce, small)


def gelu_pair(preact):
    argument = ROOT_COEF * (preact + CUBIC_COEF * preact * preact * preact)
    tanhed = jnp.tanh(argument)
    gelu_value = 0.5 * preact * (1.0 + tanhed)
    gelu_slope = 0.5 * (1.0 + tanhed) + 0.5 * preact * (1.0 - tanhed * tanhed) * ROOT_COEF * (
        1.0 + 3.0 * CUBIC_COEF * preact * preact
    )
    return (gelu_value, gelu_slope)


def contract_rows(left_side, right_side):
    return lax.dot_general(
        left_side, right_side, (((0,), (0,)), ((), ())), preferred_element_type=F32
    )


def contract_cols(left_side, right_side):
    return lax.dot_general(
        left_side, right_side, (((1,), (1,)), ((), ())), preferred_element_type=F32
    )


def shards(
    fields,
    cotangent,
    edge_match,
    depth_kernel,
    depth_bias,
    norm_gain,
    norm_bias,
    expand_weight,
    expand_bias,
    reduce_weight,
    reduce_bias,
    layer_scale,
):
    band = fields[0]
    row_count, col_count, channels = band.shape
    cells = row_count * col_count
    own_match = lax.dynamic_index_in_dim(edge_match, lax.axis_index("face"), 0, keepdims=False)
    strips, beside_side = halo(band, own_match)
    above, below, (west, east) = unpack(*exchange(band, strips, 0), own_match, beside_side)
    tall = jnp.concatenate([above, band, below], axis=0)
    padded = jnp.concatenate([jnp.flip(west, 1), tall, east], axis=1).astype(F32)
    kernel = depth_kernel.astype(F32)

    convolved = jnp.zeros((row_count, col_count, channels), F32) + depth_bias
    for row_off in range(7):
        for col_off in range(7):
            convolved = (
                convolved
                + kernel[row_off, col_off]
                * padded[row_off : row_off + row_count, col_off : col_off + col_count]
            )
    average = jnp.mean(convolved, axis=-1, keepdims=True)
    centred = convolved - average
    inverse = lax.rsqrt(jnp.mean(centred * centred, axis=-1, keepdims=True) + EPSILON)
    standard = centred * inverse
    normed = (standard * norm_gain + norm_bias).astype(BF16).reshape(cells, channels)
    preact = jnp.dot(normed, expand_weight, preferred_element_type=F32) + expand_bias
    gelu_value, gelu_slope = gelu_pair(preact)
    activated = gelu_value.astype(BF16)
    branch = jnp.dot(activated, reduce_weight, preferred_element_type=F32) + reduce_bias
    residual = band.reshape(cells, channels).astype(F32)
    result = (residual + layer_scale * branch).astype(BF16).reshape(band.shape)
    upstream = cotangent[0].reshape(cells, channels).astype(F32)
    grad_branch = (upstream * layer_scale).astype(BF16)
    grad_pre = (contract_cols(grad_branch, reduce_weight) * gelu_slope).astype(BF16)
    grad_normed = contract_cols(grad_pre, expand_weight).reshape(row_count, col_count, channels)
    scaled = grad_normed * norm_gain
    grad_conv = (
        scaled
        - jnp.mean(scaled, axis=-1, keepdims=True)
        - standard * jnp.mean(scaled * standard, axis=-1, keepdims=True)
    ) * inverse

    grad_rows = grad_conv.astype(BF16)
    strips, _ = halo(grad_rows, own_match)
    above, below, ghosts = unpack(*exchange(grad_rows, strips, 1), own_match, beside_side)
    tall = jnp.concatenate([above.astype(F32), grad_conv, below.astype(F32)], axis=0)
    tall = jnp.pad(tall, ((0, 0), (3, 3), (0, 0)))
    interior = cotangent[0].astype(F32)
    kernel_terms = []
    for row_off in range(7):
        for col_off in range(7):
            interior = (
                interior
                + kernel[row_off, col_off]
                * tall[6 - row_off : 6 - row_off + row_count, 6 - col_off : 6 - col_off + col_count]
            )
            kernel_terms.append(
                jnp.sum(
                    grad_conv
                    * padded[row_off : row_off + row_count, col_off : col_off + col_count],
                    axis=(0, 1),
                )
            )
    for side in range(2):
        taps = jnp.where(own_match[side, 2] == 1, jnp.flip(kernel, 0), kernel)
        taps = jnp.where(own_match[side, 1] == 1, taps[:, 4:7], jnp.flip(taps[:, 0:3], 1))
        ghost = ghosts[side].astype(F32)
        columns = []
        for depth in range(3):
            total = jnp.zeros((row_count, channels), F32)
            for other in range(3 - depth):
                for row_off in range(7):
                    total = (
                        total
                        + taps[row_off, depth + other]
                        * ghost[6 - row_off : 6 - row_off + row_count, other]
                    )
            columns.append(total)
        if side == 0:
            interior = interior.at[:, 0:3].add(jnp.stack(columns, 1))
        else:
            interior = interior.at[:, col_count - 3 :].add(jnp.stack(columns[::-1], 1))
    grad_fields = interior.astype(BF16)

    vectors = jnp.stack(
        [
            jnp.sum(grad_conv, axis=(0, 1)),
            jnp.sum(grad_normed * standard, axis=(0, 1)),
            jnp.sum(grad_normed, axis=(0, 1)),
            jnp.sum(upstream, axis=0) * layer_scale,
            jnp.sum(upstream * branch, axis=0),
        ]
    )
    grad_expand_bias = jnp.sum(grad_pre.astype(F32), axis=0)
    small = jnp.concatenate(
        [
            jnp.stack(kernel_terms).reshape(-1),
            grad_expand_bias,
            vectors.reshape(-1),
            jnp.zeros((6 * 256,), F32),
        ]
    ).reshape(4, 4, 8, 128)
    grad_expand = contract_rows(normed, grad_pre)
    grad_reduce = contract_rows(activated, grad_branch)
    scale = 1.0 / math.sqrt(FACES * TILES * cells)
    grad_expand, grad_reduce, small = reduce_all(grad_expand, grad_reduce, small, scale)
    small = small.reshape(-1)
    return (
        result[None],
        grad_fields[None],
        small[: 49 * 256].reshape(7, 7, 256),
        grad_expand,
        grad_reduce,
        small[49 * 256 : 53 * 256],
        small[53 * 256 : 58 * 256].reshape(5, 256),
    )


def solution(mesh):
    return jax.shard_map(
        shards,
        mesh=mesh,
        in_specs=(P("face", "tile", None, None),) * 2 + (P(),) * 10,
        out_specs=(P("face", "tile", None, None),) * 2 + (P(),) * 5,
        check_vma=False,
    )
```

time: 506 us -> 157 us (0.31)
  waiting for transfers between devices: 249 us -> 0 us
  blocking collectives: 131 us -> 0 us
  Pallas kernels: 0 us -> 80.5 us
  starting transfers between devices: 34.9 us -> 0 us
  between operations: 20.8 us -> 6.06 us
  local copies, waits for them, and re-layouts: 8.93 us -> 17.4 us
  other arithmetic: 46 us -> 38.2 us
    psum x1 -> x0, waiting for transfers between devices: 228 us -> none  [shards(): lax.psum((grad_kernel, grad_expand, grad_reduce, grad_expand_bias, vector...]
    psum x1 -> x0, blocking collectives: 83.3 us -> none  [shards(): lax.psum((grad_kernel, grad_expand, grad_reduce, grad_expand_bias, vector...]
    pallas_call x0 -> x3, Pallas kernels: none -> 80.5 us  [the longest x1 43.3 us: reduce_all(): pl.pallas_call(functools.partial(reduce_kernel, scale=scale), out_shape=(...]
    all_gather x2 -> x0, blocking collectives: 47.4 us -> none  [the longest x1 23.9 us: partner_strips(): gathered = lax.all_gather(both_kinds[None], 'face', axis=0, tiled=True)]
    ppermute x14 -> x0, starting transfers between devices: 34.9 us -> none  [the longest x10 16.3 us: swapped(): lax.ppermute(x, axis, [(i, i ^ 1 << stride) for i in range(lax.axis_size(...]
    ppermute x14 -> x0, waiting for transfers between devices: 21 us -> none  [the longest x10 14.6 us: swapped(): lax.ppermute(x, axis, [(i, i ^ 1 << stride) for i in range(lax.axis_size(...]
    another operation x6 -> x0, other arithmetic: 17.5 us -> none
    add x2 -> x7, other arithmetic: 0.03 us -> 9.44 us  [the longest x1 9.25 us: shards(): interior + kernel[row_off, col_off] * tall[6 - row_off:6 - row_off + row_...]
  transfers between devices with their start and end apart: 15 -> 0, of which waited for: 10 -> 0; matrix products, arithmetic and copies ran while one was open for 3% -> 0% of each run, Pallas kernels for 0% -> 0%
where the time goes in v1:
time: 157 us
  Pallas kernels  80.5 us (51%)
  other arithmetic  38.2 us (24%)
  local copies, waits for them, and re-layouts  17.4 us (11%)
  matrix products  14.4 us (9%)
  between operations  6.06 us (4%)
    pallas_call x1, Pallas kernels, reduce_all(): pl.pallas_call(functools.partial(reduce_kernel, scale=scale), out_shape=(...  43.3 us
    pallas_call x2, Pallas kernels, exchange(): pl.pallas_call(halo_kernel, out_shape=(jax.ShapeDtypeStruct((3, col_count...  37.2 us
    reduce_sum x3, other arithmetic, shards(): jnp.sum(grad_conv * padded[row_off:row_off + row_count, col_off:col_off +...  10.3 us
    reduce_sum x1, other arithmetic, shards(): average = jnp.mean(convolved, axis=-1, keepdims=True)  9.51 us
    add x1, other arithmetic, shards(): interior + kernel[row_off, col_off] * tall[6 - row_off:6 - row_off + row_...  9.25 us
    unnamed x256, local copies, waits for them, and re-layouts  6.41 us
    dot_general x2, matrix products, contract_rows(): lax.dot_general(left_side, right_side, (((0,), (0,)), ((), ())), preferre...  5.24 us
    dot_general x2, matrix products, contract_cols(): lax.dot_general(left_side, right_side, (((1,), (1,)), ((), ())), preferre...  5.15 us

profile of v1, /device:TPU:1, one launch (start us, length us, event | category | flops | bytes accessed | tf_op | source)
XLA Modules:
  0.0 156.5 jit_solution(3993579659316540471)
XLA Ops:
  2.9 1.3 copy.78
  4.8 21.3 %shard_map.171 = (bf16[3,128,256]{2,1,0:T(8,128)(2,1)}, bf16[3,128,256]{2,1,0:T(8,128)(2,1)}, bf16[2,2,3,3,8,256]{5,4,3,2,1,0:T(8,128)(2,1)}) custom-call(bf16[8,128,256]{2,1,0:T(8,128)(2,1)} %bitcast.270, bf16[2,3,8,256]{3,2,1,0:T(8,128)(2,1)} %maximum_select_fusion.strips_ref), custom_call_target="tpu_custom_call" | custom-call | tf_op jit(solution)/shard_map/pallas_call | solution.py:72
  26.1 0.9 slice_bitcast_fusion.3
  29.0 1.4 copy_select_fusion.2
  32.0 9.5 %fusion.100 = (f32[8,128]{0,1:T(8,128)S(1)}, f32[8,128,256]{2,0,1:T(8,128)S(1)}) fusion(f32[14,134,256]{2,0,1:T(8,128)S(1)} %maximum_convert_fusion, f32[256]{0:T(256)} %bitcast.73, f32[256]{0:T(256)} %bitcast.72, f32[256]{0:T(256)} %bitcast.71, f32[256]{0:T(256)} %bitcast.70, f32[256]{0:T(256)} %bitcast.69, f32[256]{0:T(256)} %bitcast.68, f32[256]{0:T(256)} %bitcast.67, ...), kind=kLoop, calls=%fused_computation.291 | loop fusion | flops 25951232 | bytes 52484096 | tf_op jit(solution)/shard_map/reduce_sum | solution.py:438
  42.9 1.8 %multiply_convert_fusion = (bf16[1024,1024]{1,0:T(8,128)(2,1)S(1)}, f32[1024,1024]{1,0:T(8,128)S(1)}) fusion(f32[1024]{0:T(1024)S(1)} %copy-done.122, bf16[1024,256]{1,0:T(8,128)(2,1)S(1)} %bitcast.268, bf16[256,1024]{1,0:T(8,128)(2,1)S(1)} %copy-done), kind=kOutput, calls=%fused_computation.10 | convolution fusion | flops 547356672 | bytes 7344128 | tf_op jit(solution)/shard_map/dot_general | solution.py:443
  46.7 2.2 %fusion.69 = (f32[256]{0:T(256)}, bf16[1024,256]{1,0:T(8,128)(2,1)S(1)}, bf16[1024,256]{1,0:T(8,128)(2,1)}) fusion(f32[1,8,128,256]{3,2,1,0:T(8,128)S(1)} %copy.42, f32[256]{0:T(256)S(1)} %copy-done.116, bf16[1,8,128,256]{3,2,1,0:T(8,128)(2,1)S(1)} %copy-done.11, f32[256]{0:T(256)S(1)} %copy-done.123, bf16[1024,1024]{1,0:T(8,128)(2,1)S(1)} %get-tuple-element.246, ...), kind=kOutput, calls=%fused_computation.134 | convolution fusion | flops 539229952 | bytes 5245952 | tf_op jit(solution)/shard_map/dot_general | solution.py:446
  48.9 3.8 %convert_reduce_fusion = (f32[1024]{0:T(1024)}, bf16[1024,1024]{1,0:T(8,128)(2,1)S(1)}) fusion(f32[1024,1024]{1,0:T(8,128)S(1)} %get-tuple-element.247, f32[1024]{0:T(1024)S(1)} %copy-done.122, bf16[1024,256]{1,0:T(8,128)(2,1)S(1)} %get-tuple-element.122, bf16[1024,256]{1,0:T(8,128)(2,1)S(1)} %copy-done.121), kind=kOutput, calls=%fused_computation.9 | convolution fusion | flops 559938560 | bytes 7348224 | tf_op jit(solution)/shard_map/dot_general | solution.py:401
  52.8 1.3 fusion.99
  54.1 1.3 multiply_reduce_fusion
  55.6 5.7 %multiply_reduce_fusion.1 = (f32[256]{0:T(256)S(1)}, f32[256]{0:T(256)}, f32[256]{0:T(256)}, f32[256]{0:T(256)}, f32[256]{0:T(256)}, /*index=5*/f32[256]{0:T(256...) fusion(f32[14,134,256]{2,0,1:T(8,128)S(1)} %maximum_convert_fus, ...), kind=kLoop, calls=%fused_computation.136 | loop fusion | flops 11267584 | bytes 22055936 | tf_op jit(solution)/shard_map/reduce_sum | solution.py:475
  61.3 1.4 multiply_reduce_fusion.37
  62.9 3.2 %multiply_reduce_fusion.19 = (f32[256]{0:T(256)S(1)}, f32[256]{0:T(256)S(1)}, f32[256]{0:T(256)S(1)}, f32[256]{0:T(256)S(1)}, f32[256]{0:T(256)S(1)}, /*index=5*...) fusion(f32[8,128,256]{2,0,1:T(8,128)S(1)} %get-tuple-element.11, ...), kind=kLoop, calls=%fused_computation.154 | loop fusion | flops 9694720 | bytes 20465664 | tf_op jit(solution)/shard_map/reduce_sum | solution.py:475
  67.5 3.5 %fusion.112.reduce_ref = f32[1024,256]{1,0:T(8,128)} fusion(bf16[1024,1024]{1,0:T(8,128)(2,1)} %copy-done.124, bf16[1024,256]{1,0:T(8,128)(2,1)} %copy-done.125), kind=kOutput, calls=%fused_computation.303 | convolution fusion | flops 536870912 | bytes 3670016 | tf_op jit(solution)/shard_map/dot_general | solution.py:395
  71.1 1.7 %fusion.111.expand_ref = f32[256,1024]{1,0:T(8,128)} fusion(bf16[1024,256]{1,0:T(8,128)(2,1)S(1)} %bitcast.269, bf16[1024,1024]{1,0:T(8,128)(2,1)S(1)} %copy-done.8), kind=kOutput, calls=%fused_computation.302 | convolution fusion | flops 536870912 | bytes 3670016 | tf_op jit(solution)/shard_map/dot_general | solution.py:395
  72.8 43.3 %shard_map.173 = (f32[256,1024]{1,0:T(8,128)}, f32[1024,256]{1,0:T(8,128)}, f32[4,4,8,128]{3,2,1,0:T(8,128)}) custom-call(f32[256,1024]{1,0:T(8,128)} %fusion.111.expand_ref, f32[1024,256]{1,0:T(8,128)} %fusion.112.reduce_ref, f32[4,4,8,128]{3,2,1,0:T(8,128)} %bitcast.271), custom_call_target="tpu_custom_call" | custom-call | tf_op jit(solution)/shard_map/pallas_call | solution.py:350
  119.0 1.3 slice.1626
  121.8 15.9 %shard_map.172 = (bf16[3,128,256]{2,1,0:T(8,128)(2,1)}, bf16[3,128,256]{2,1,0:T(8,128)(2,1)}, bf16[2,2,3,3,8,256]{5,4,3,2,1,0:T(8,128)(2,1)}) custom-call(bf16[8,128,256]{2,1,0:T(8,128)(2,1)} %copy.45.rows_ref, bf16[2,3,8,256]{3,2,1,0:T(8,128)(2,1)} %maximum_select_fusion.1.strips_ref), custom_call_target="tpu_custom_call" | custom-call | tf_op jit(solution)/shard_map/pallas_call | solution.py:72
  137.7 1.0 slice_bitcast_fusion.1
  141.8 1.7 %select_maximum_fusion = f32[14,134,256]{2,0,1:T(8,128)S(1)} fusion(f32[3,128,256]{2,0,1:T(4,128)S(1)} %fusion.71, f32[8,128,256]{2,0,1:T(8,128)} %copy-done.2, f32[3,128,256]{2,0,1:T(4,128)S(1)} %fusion.72), kind=kLoop, calls=%fused_computation.21 | loop fusion | flops 3842048 | bytes 3756032 | tf_op jit(solution)/shard_map/concatenate | solution.py:463
  143.9 9.3 %fusion.20 = f32[8,128,256]{2,0,1:T(8,128)S(1)} fusion(f32[8,128,256]{2,0,1:T(8,128)S(1)} %copy-done.3, f32[3,128,256]{2,0,1:T(4,128)S(1)} %fusion.72, f32[3,128,256]{2,0,1:T(4,128)S(1)} %fusion.71, f32[14,134,256]{2,0,1:T(8,128)S(1)} %select_maximum_fusion, f32[256]{0:T(256)} %bitcast.73, f32[256]{0:T(256)} %bitcast.72, f32[256]{0:T(256)} %bitcast.71, ...), kind=kLoop, calls=%fused_computation.38 | loop fusion | flops 27525120 | bytes 47498240 | tf_op jit(solution)/shard_map/add | solution.py:470
  153.3 0.9 copy.51
  154.6 1.0 copy.83
  155.6 1.0 copy.84
  (330 shorter events, 14.7 us)
Async XLA Ops:
  0.6 42.2 %copy-start = (bf16[256,1024]{1,0:T(8,128)(2,1)S(1)}, bf16[256,1024]{1,0:T(8,128)(2,1)}, u32[]{:S(2)}) copy-start(bf16[256,1024]{1,0:T(8,128)(2,1)} %param.23) | copy-start | bytes 1572868
  31.0 10.6 %copy-start.17 = (f32[1,1,256]{2,1,0:T(1,128)}, f32[1,1,256]{2,1,0:T(1,128)S(1)}, u32[]{:S(2)}) copy-start(f32[1,1,256]{2,1,0:T(1,128)S(1)} %get-tuple-element.192) | copy-start | bytes 3076
  31.0 10.6 %copy-start.19 = (f32[1,1,256]{2,1,0:T(1,128)}, f32[1,1,256]{2,1,0:T(1,128)S(1)}, u32[]{:S(2)}) copy-start(f32[1,1,256]{2,1,0:T(1,128)S(1)} %get-tuple-element.193) | copy-start | bytes 3076
  31.0 10.6 %copy-start.21 = (f32[1,1,256]{2,1,0:T(1,128)}, f32[1,1,256]{2,1,0:T(1,128)S(1)}, u32[]{:S(2)}) copy-start(f32[1,1,256]{2,1,0:T(1,128)S(1)} %get-tuple-element.194) | copy-start | bytes 3076
  31.0 10.6 %copy-start.23 = (f32[1,1,256]{2,1,0:T(1,128)}, f32[1,1,256]{2,1,0:T(1,128)S(1)}, u32[]{:S(2)}) copy-start(f32[1,1,256]{2,1,0:T(1,128)S(1)} %get-tuple-element.195) | copy-start | bytes 3076
  31.0 10.6 %copy-start.25 = (f32[1,1,256]{2,1,0:T(1,128)}, f32[1,1,256]{2,1,0:T(1,128)S(1)}, u32[]{:S(2)}) copy-start(f32[1,1,256]{2,1,0:T(1,128)S(1)} %get-tuple-element.196) | copy-start | bytes 3076
  31.1 10.6 %copy-start.27 = (f32[1,1,256]{2,1,0:T(1,128)}, f32[1,1,256]{2,1,0:T(1,128)S(1)}, u32[]{:S(2)}) copy-start(f32[1,1,256]{2,1,0:T(1,128)S(1)} %get-tuple-element.197) | copy-start | bytes 3076
  31.1 10.6 %copy-start.29 = (f32[1,1,256]{2,1,0:T(1,128)}, f32[1,1,256]{2,1,0:T(1,128)S(1)}, u32[]{:S(2)}) copy-start(f32[1,1,256]{2,1,0:T(1,128)S(1)} %get-tuple-element.198) | copy-start | bytes 3076
  31.1 10.6 %copy-start.31 = (f32[1,1,256]{2,1,0:T(1,128)}, f32[1,1,256]{2,1,0:T(1,128)S(1)}, u32[]{:S(2)}) copy-start(f32[1,1,256]{2,1,0:T(1,128)S(1)} %get-tuple-element.199) | copy-start | bytes 3076
  31.1 10.6 %copy-start.33 = (f32[1,1,256]{2,1,0:T(1,128)}, f32[1,1,256]{2,1,0:T(1,128)S(1)}, u32[]{:S(2)}) copy-start(f32[1,1,256]{2,1,0:T(1,128)S(1)} %get-tuple-element.200) | copy-start | bytes 3076
  31.1 10.6 %copy-start.35 = (f32[1,1,256]{2,1,0:T(1,128)}, f32[1,1,256]{2,1,0:T(1,128)S(1)}, u32[]{:S(2)}) copy-start(f32[1,1,256]{2,1,0:T(1,128)S(1)} %get-tuple-element.201) | copy-start | bytes 3076
  31.1 10.6 %copy-start.37 = (f32[1,1,256]{2,1,0:T(1,128)}, f32[1,1,256]{2,1,0:T(1,128)S(1)}, u32[]{:S(2)}) copy-start(f32[1,1,256]{2,1,0:T(1,128)S(1)} %get-tuple-element.202) | copy-start | bytes 3076
  31.1 10.6 %copy-start.39 = (f32[1,1,256]{2,1,0:T(1,128)}, f32[1,1,256]{2,1,0:T(1,128)S(1)}, u32[]{:S(2)}) copy-start(f32[1,1,256]{2,1,0:T(1,128)S(1)} %get-tuple-element.203) | copy-start | bytes 3076
  31.1 10.6 %copy-start.41 = (f32[1,1,256]{2,1,0:T(1,128)}, f32[1,1,256]{2,1,0:T(1,128)S(1)}, u32[]{:S(2)}) copy-start(f32[1,1,256]{2,1,0:T(1,128)S(1)} %get-tuple-element.204) | copy-start | bytes 3076
  31.1 10.6 %copy-start.43 = (f32[1,1,256]{2,1,0:T(1,128)}, f32[1,1,256]{2,1,0:T(1,128)S(1)}, u32[]{:S(2)}) copy-start(f32[1,1,256]{2,1,0:T(1,128)S(1)} %get-tuple-element.205) | copy-start | bytes 3076
  31.1 10.6 %copy-start.45 = (f32[1,1,256]{2,1,0:T(1,128)}, f32[1,1,256]{2,1,0:T(1,128)S(1)}, u32[]{:S(2)}) copy-start(f32[1,1,256]{2,1,0:T(1,128)S(1)} %get-tuple-element.206) | copy-start | bytes 3076
  31.2 10.5 %copy-start.47 = (f32[1,1,256]{2,1,0:T(1,128)}, f32[1,1,256]{2,1,0:T(1,128)S(1)}, u32[]{:S(2)}) copy-start(f32[1,1,256]{2,1,0:T(1,128)S(1)} %get-tuple-element.207) | copy-start | bytes 3076
  31.2 10.5 %copy-start.49 = (f32[1,1,256]{2,1,0:T(1,128)}, f32[1,1,256]{2,1,0:T(1,128)S(1)}, u32[]{:S(2)}) copy-start(f32[1,1,256]{2,1,0:T(1,128)S(1)} %get-tuple-element.208) | copy-start | bytes 3076
  31.2 10.5 %copy-start.51 = (f32[1,1,256]{2,1,0:T(1,128)}, f32[1,1,256]{2,1,0:T(1,128)S(1)}, u32[]{:S(2)}) copy-start(f32[1,1,256]{2,1,0:T(1,128)S(1)} %get-tuple-element.209) | copy-start | bytes 3076
  31.2 10.5 %copy-start.53 = (f32[1,1,256]{2,1,0:T(1,128)}, f32[1,1,256]{2,1,0:T(1,128)S(1)}, u32[]{:S(2)}) copy-start(f32[1,1,256]{2,1,0:T(1,128)S(1)} %get-tuple-element.210) | copy-start | bytes 3076
  31.2 10.5 %copy-start.55 = (f32[1,1,256]{2,1,0:T(1,128)}, f32[1,1,256]{2,1,0:T(1,128)S(1)}, u32[]{:S(2)}) copy-start(f32[1,1,256]{2,1,0:T(1,128)S(1)} %get-tuple-element.211) | copy-start | bytes 3076
  41.9 12.2 %copy-start.1 = (f32[8,128,256]{2,0,1:T(8,128)}, f32[8,128,256]{2,0,1:T(8,128)S(1)}, u32[]{:S(2)}) copy-start(f32[8,128,256]{2,0,1:T(8,128)S(1)} %get-tuple-element.119) | copy-start | bytes 3145732
  71.1 49.2 %copy-start.6 = (bf16[8,128,256]{2,0,1:T(8,128)(2,1)S(1)}, bf16[8,128,256]{2,0,1:T(8,128)(2,1)}, u32[]{:S(2)}) copy-start(bf16[8,128,256]{2,0,1:T(8,128)(2,1)} %get-tuple-element.120) | copy-start | bytes 1572868
  72.8 66.4 %copy-start.114 = (pred[14]{0:T(512)(128)(4,1)S(1)}, pred[14]{0:T(512)(128)(4,1)}, u32[]{:S(2)}) copy-start(pred[14]{0:T(512)(128)(4,1)} %copy-done.113) | copy-start | bytes 46
  (102 other events, 416.7 us)

commit v2 on v1

v2 whole, which is shorter than its diff:
```python
import functools
import math

import jax
import jax.numpy as jnp
from jax import lax
from jax.experimental import pallas as pl
from jax.experimental.pallas import tpu as pltpu
from jax.sharding import PartitionSpec as P

EPSILON = 1e-06
ROOT_COEF = 0.7978845608028654
CUBIC_COEF = 0.044715
MESH = pl.DeviceIdType.MESH
FACES = 8
TILES = 32
ROWS = 8
COLS = 128
CH = 256
HID = 1024
F32 = jnp.float32
BF16 = jnp.bfloat16
OWN_PAIRS = [(i, a) for i in range(ROWS) for a in range(7) if 3 <= i + a <= 10]
RIM_PAIRS = [(i, a) for i in range(ROWS) for a in range(7) if not 3 <= i + a <= 10]


def halo_plan(face, tile):
    beside = face + 1 - 2 * lax.rem(face, 2)
    across = lax.rem(face + 4, FACES)
    plan = [
        ("up", (face, lax.rem(tile + TILES - 1, TILES))),
        ("down", (face, lax.rem(tile + 1, TILES))),
    ]
    for link, partner in enumerate((beside, across)):
        for flip in range(2):
            for place in range(3):
                if flip == 0:
                    target = tile + TILES + 1 - place
                else:
                    target = 2 * TILES - tile - place
                plan.append(((link, flip, place), (partner, lax.rem(target, TILES))))
    return plan


def device_at(x, y, z, core):
    return (2 * y + lax.rem(x, 2), 16 * lax.div(x, 2) + 2 * z + core)


def pick(flag, if_one, if_zero):
    return jnp.where(jnp.broadcast_to(flag, if_one.shape) == 1, if_one, if_zero)


def dot_nn(left, right):
    return lax.dot_general(left, right, (((1,), (0,)), ((), ())), preferred_element_type=F32)


def dot_nt(left, right):
    return lax.dot_general(left, right, (((1,), (1,)), ((), ())), preferred_element_type=F32)


def fold(block):
    return jnp.sum(block.reshape(16, 8, block.shape[1]), axis=0)


def conv_chunk(shifted, taps, flipped, out, chunk, pairs, start):
    cols = pl.ds(pl.multiple_of(chunk * 8, 8), 8)
    for half in range(2):
        lanes = slice(half * 128, half * 128 + 128)
        acc = {}
        for i in sorted({i for i, _ in pairs}):
            acc[i] = out[i, cols, lanes] if start is None else start[:, lanes]
        for b in range(7):
            rows = {r: shifted[b, r, cols, lanes] for r in sorted({i + a for i, a in pairs})}
            for a in sorted({a for _, a in pairs}):
                tap = taps[48 - a * 7 - b if flipped else a * 7 + b, :, lanes]
                for i in sorted({i for i, a2 in pairs if a2 == a}):
                    acc[i] = acc[i] + tap * rows[i + a]
        for i, value in acc.items():
            out[i, cols, lanes] = value


def block_kernel(
    edge_ref,
    fields_ref,
    cot_ref,
    taps_ref,
    depth_bias_ref,
    gain_ref,
    norm_bias_ref,
    w1_ref,
    b1_ref,
    w2_ref,
    b2_ref,
    scale_ref,
    result_ref,
    gfields_ref,
    gkernel_ref,
    gexpand_ref,
    greduce_ref,
    gbias_ref,
    gvectors_ref,
    taps,
    wide,
    shifted,
    shifted_g,
    strip_f,
    strips,
    above,
    below,
    ghosts,
    ghost_f,
    rows_g,
    strips_g,
    above_g,
    below_g,
    ghosts_g,
    conv,
    standard,
    inverse,
    normed,
    normed_t,
    cot_branch_t,
    grad_hidden,
    active,
    grad_pre,
    bias_sum,
    vector_sum,
    src,
    from_core,
    sum_core,
    from_a,
    sum_a,
    from_b,
    sum_b,
    from_z,
    gathered,
    small_in,
    small_core,
    small_sum,
    small_x,
    small_sum_x,
    small_y,
    small_z,
    small_out,
    halo_send,
    halo_recv,
    grad_send,
    grad_recv,
    big_send,
    big_recv,
    small_send,
    small_recv,
    factor,
):
    face, tile = lax.axis_index("face"), lax.axis_index("tile")
    core = lax.rem(tile, 2)
    z = lax.rem(lax.div(tile, 2), 8)
    x = 2 * lax.div(tile, 16) + lax.rem(face, 2)
    y = lax.div(face, 2)
    sibling = device_at(x, y, z, 1 - core)

    def x_peer(step):
        return device_at(lax.rem(x + step, 4), y, z, core)

    def y_peer(step):
        return device_at(x, lax.rem(y + step, 4), z, core)

    def z_peer(step):
        return device_at(x, y, lax.rem(z + step, 8), core)

    place_a = x + core * (y - x)
    place_b = y + core * (x - y)

    def a_peer(step):
        new = lax.rem(place_a + step, 4)
        return device_at(new + core * (x - new), y + core * (new - y), z, core)

    def b_peer(step):
        new = lax.rem(place_b + step, 4)
        return device_at(x + core * (new - x), new + core * (y - new), z, core)

    plan = halo_plan(face, tile)
    barrier = pltpu.get_barrier_semaphore()
    peers = [target for _, target in plan]
    peers += [sibling]
    peers += [x_peer(step) for step in range(1, 4)]
    peers += [y_peer(step) for step in range(1, 4)]
    peers += [z_peer(step) for step in range(1, 8)]
    for peer in peers:
        pl.semaphore_signal(barrier, inc=1, device_id=peer, device_id_type=MESH)

    first = jnp.where(tile == 0, 1, 0)
    last = jnp.where(tile == TILES - 1, 1, 0)
    beside = face + 1 - 2 * lax.rem(face, 2)
    beside_side = jnp.where(edge_ref[face * 6] == beside, 0, 1)

    def make_strips(target):
        for row in range(ROWS):
            for depth in range(3):
                for side, col in ((0, 8 + depth), (1, 135 - depth)):
                    piece = wide[3 + row, col : col + 1, :]
                    strip_f[side, 0, depth, row : row + 1, :] = piece
                    strip_f[side, 1, depth, 7 - row : 8 - row, :] = piece
        for flip in range(2):
            for depth in range(3):
                west, east = strip_f[0, flip, depth], strip_f[1, flip, depth]
                target[0, flip, depth] = pick(beside_side, east, west).astype(BF16)
                target[1, flip, depth] = pick(beside_side, west, east).astype(BF16)

    def start_halo(rows, strip, to_above, to_below, to_ghosts, send, recv):
        copies = []
        for index, (kind, target) in enumerate(plan):
            if kind == "up":
                source, landing = rows.at[0:3], to_below
            elif kind == "down":
                source, landing = rows.at[ROWS - 3 : ROWS], to_above
            else:
                link, flip, place = kind
                source, landing = strip.at[link, flip], to_ghosts.at[link, flip, place]
            copy = pltpu.make_async_remote_copy(
                source, landing, send.at[index], recv.at[index], target, MESH
            )
            copy.start()
            copies.append(copy)
        return copies

    def take_ghosts(source):
        for side in range(2):
            reverse = edge_ref[face * 6 + side * 3 + 2]
            other = beside_side if side == 0 else 1 - beside_side
            for place in range(3):
                for depth in range(3):
                    values = [
                        pick(
                            other,
                            source[1, flip, place, depth].astype(F32),
                            source[0, flip, place, depth].astype(F32),
                        )
                        for flip in range(2)
                    ]
                    value = pick(reverse, values[1], values[0])
                    if place == 0:
                        value = pick(first, jnp.zeros_like(value), value)
                    if place == 2:
                        value = pick(last, jnp.zeros_like(value), value)
                    ghost_f[side, depth, place * 8 : place * 8 + 8, :] = value

    def take_rows(source_above, source_below):
        for row in range(3):
            value = source_above[row].astype(F32)
            wide[row, 8:136, :] = pick(first, jnp.zeros_like(value), value)
            value = source_below[row].astype(F32)
            wide[11 + row, 8:136, :] = pick(last, jnp.zeros_like(value), value)

    def shift_row(target, row):
        for b in range(7):
            target[b, row] = wide[row, 5 + b : 133 + b, :]

    for a in range(7):
        block = taps_ref[a].astype(F32)
        for b in range(7):
            taps[a * 7 + b] = jnp.broadcast_to(block[b : b + 1, :], (8, CH))
    edge_zero = jnp.zeros((8, CH), F32)

    def load_row(row, carry):
        wide[3 + row, 0:8, :] = edge_zero
        wide[3 + row, 136:144, :] = edge_zero
        wide[3 + row, 8:136, :] = fields_ref[row].astype(F32)
        return carry

    lax.fori_loop(0, ROWS, load_row, 0)
    make_strips(strips)
    vector_sum[...] = jnp.zeros_like(vector_sum)
    bias_sum[...] = jnp.zeros_like(bias_sum)

    def own_shift(row, carry):
        shift_row(shifted, 3 + row)
        return carry

    lax.fori_loop(0, ROWS, own_shift, 0)
    pl.semaphore_wait(barrier, len(peers))
    halo = start_halo(fields_ref, strips, above, below, ghosts, halo_send, halo_recv)

    def cot_row(row, carry):
        cells = pl.ds(pl.multiple_of(row * COLS, COLS), COLS)
        upstream = cot_ref[row].astype(F32)
        scaled = upstream * scale_ref[...]
        branch_grad = scaled.astype(BF16)
        cot_branch_t[:, cells] = jnp.transpose(scaled).astype(BF16)
        vector_sum[3] = vector_sum[3] + fold(upstream)
        for part in range(4):
            hidden = slice(part * 256, part * 256 + 256)
            grad_hidden[cells, hidden] = dot_nt(branch_grad, w2_ref[hidden, :])
        return carry

    lax.fori_loop(0, ROWS, cot_row, 0)
    start = jnp.broadcast_to(depth_bias_ref[...], (8, CH))

    def own_conv(chunk, carry):
        conv_chunk(shifted, taps, False, conv, chunk, OWN_PAIRS, start)
        return carry

    lax.fori_loop(1, 15, own_conv, 0)
    for copy in halo:
        copy.wait()

    take_ghosts(ghosts)
    take_rows(above, below)
    for row in range(14):
        for depth in range(3):
            wide[row, 7 - depth : 8 - depth, :] = ghost_f[0, depth, row + 5 : row + 6, :]
            wide[row, 136 + depth : 137 + depth, :] = ghost_f[1, depth, row + 5 : row + 6, :]

    def rim_shift(row, carry):
        shift_row(shifted, row)
        shift_row(shifted, 11 + row)
        return carry

    lax.fori_loop(0, 3, rim_shift, 0)

    def edge_shift(row, carry):
        for b in range(7):
            shifted[b, 3 + row, 0:8, :] = wide[3 + row, 5 + b : 13 + b, :]
            shifted[b, 3 + row, 120:128, :] = wide[3 + row, 125 + b : 133 + b, :]
        return carry

    lax.fori_loop(0, ROWS, edge_shift, 0)

    def rim_conv(chunk, carry):
        conv_chunk(shifted, taps, False, conv, chunk, RIM_PAIRS, None)
        return carry

    lax.fori_loop(1, 15, rim_conv, 0)

    def edge_conv(index, carry):
        conv_chunk(shifted, taps, False, conv, index * 15, OWN_PAIRS + RIM_PAIRS, start)
        return carry

    lax.fori_loop(0, 2, edge_conv, 0)

    def norm_row(row, carry):
        cells = pl.ds(pl.multiple_of(row * COLS, COLS), COLS)
        value = conv[row]
        centred = value - jnp.sum(value, axis=1, keepdims=True) * (1.0 / CH)
        variance = jnp.sum(centred * centred, axis=1, keepdims=True) * (1.0 / CH)
        inv = lax.rsqrt(variance + EPSILON)
        std = centred * inv
        standard[row] = std
        inverse[row] = inv
        scaled = std * gain_ref[...] + norm_bias_ref[...]
        block = scaled.astype(BF16)
        normed[cells, :] = block
        normed_t[:, cells] = jnp.transpose(scaled).astype(BF16)
        for part in range(4):
            hidden = slice(part * 256, part * 256 + 256)
            pre = dot_nn(block, w1_ref[:, hidden]) + b1_ref[:, hidden]
            square = pre * pre
            tanhed = jnp.tanh(pre * (ROOT_COEF + (ROOT_COEF * CUBIC_COEF) * square))
            half_pre = 0.5 * pre
            plus = 1.0 + tanhed
            active[cells, hidden] = (half_pre * plus).astype(BF16)
            slope = 0.5 * plus + (half_pre * (1.0 - tanhed * tanhed)) * (
                ROOT_COEF + (3.0 * ROOT_COEF * CUBIC_COEF) * square
            )
            grad = (grad_hidden[cells, hidden] * slope).astype(BF16)
            grad_pre[cells, hidden] = grad
            bias_sum[:, hidden] = bias_sum[:, hidden] + fold(grad.astype(F32))
        return carry

    lax.fori_loop(0, ROWS, norm_row, 0)

    def expand_part(part, carry):
        hidden = pl.ds(pl.multiple_of(part * 256, 256), 256)
        block = dot_nn(normed_t[...], grad_pre[:, hidden]).astype(BF16)
        for row in range(16):
            for col in range(2):
                src[0, row * 8 + part * 2 + col] = block[
                    row * 16 : row * 16 + 16, col * 128 : col * 128 + 128
                ]
        return carry

    def reduce_part(part, carry):
        hidden = pl.ds(pl.multiple_of(part * 256, 256), 256)
        block = jnp.transpose(dot_nn(cot_branch_t[...], active[:, hidden])).astype(BF16)
        for row in range(16):
            for col in range(2):
                src[1, part * 32 + row * 2 + col] = block[
                    row * 16 : row * 16 + 16, col * 128 : col * 128 + 128
                ]
        return carry

    lax.fori_loop(0, 4, expand_part, 0)
    lax.fori_loop(0, 4, reduce_part, 0)

    counters = [0, 0]

    def big(source, landing, target):
        index = counters[0]
        counters[0] += 1
        copy = pltpu.make_async_remote_copy(
            source, landing, big_send.at[index], big_recv.at[index], target, MESH
        )
        copy.start()
        return copy

    def small(source, landing, target):
        index = counters[1]
        counters[1] += 1
        copy = pltpu.make_async_remote_copy(
            source, landing, small_send.at[index], small_recv.at[index], target, MESH
        )
        copy.start()
        return copy

    def finish(copies):
        for copy in copies:
            copy.wait()

    big_copies = [big(src.at[1 - core], from_core, sibling)]

    def grad_row(row, carry):
        cells = pl.ds(pl.multiple_of(row * COLS, COLS), COLS)
        grad_normed = dot_nt(grad_pre[cells, :], w1_ref[...])
        std = standard[row]
        scaled = grad_normed * gain_ref[...]
        mean = jnp.sum(scaled, axis=1, keepdims=True) * (1.0 / CH)
        slant = jnp.sum(scaled * std, axis=1, keepdims=True) * (1.0 / CH)
        grad = (scaled - mean - std * slant) * inverse[row]
        conv[row] = grad
        wide[3 + row, 0:8, :] = edge_zero
        wide[3 + row, 136:144, :] = edge_zero
        wide[3 + row, 8:136, :] = grad
        rows_g[row] = grad.astype(BF16)
        vector_sum[0] = vector_sum[0] + fold(grad)
        vector_sum[1] = vector_sum[1] + fold(grad_normed * std)
        vector_sum[2] = vector_sum[2] + fold(grad_normed)
        return carry

    lax.fori_loop(0, ROWS, grad_row, 0)
    make_strips(strips_g)
    halo = start_halo(rows_g, strips_g, above_g, below_g, ghosts_g, grad_send, grad_recv)

    finish(big_copies)

    def add_core(index, carry):
        sum_core[index] = (src[core, index].astype(F32) + from_core[index].astype(F32)).astype(BF16)
        return carry

    lax.fori_loop(0, 128, add_core, 0, unroll=8)
    big_copies = []
    for step in range(1, 4):
        chunk = lax.rem(place_a + step, 4)
        big_copies.append(
            big(sum_core.at[pl.ds(chunk * 32, 32)], from_a.at[step - 1], a_peer(step))
        )

    def result_row(row, carry):
        cells = pl.ds(pl.multiple_of(row * COLS, COLS), COLS)
        branch = dot_nn(active[cells, :], w2_ref[...]) + b2_ref[...]
        result_ref[row] = (fields_ref[row].astype(F32) + scale_ref[...] * branch).astype(BF16)
        vector_sum[4] = vector_sum[4] + fold(cot_ref[row].astype(F32) * branch)
        return carry

    lax.fori_loop(0, ROWS, result_row, 0)

    small_in[...] = jnp.zeros_like(small_in)
    for b in range(7):

        def tap_sums(chunk, carry):
            cols = pl.ds(pl.multiple_of(chunk * 8, 8), 8)
            sums = list(carry)
            for half in range(2):
                lanes = slice(half * 128, half * 128 + 128)
                grads = [conv[i, cols, lanes] for i in range(ROWS)]
                for r in range(14):
                    value = shifted[b, r, cols, lanes]
                    for a in range(7):
                        if 0 <= r - a < ROWS:
                            sums[a * 2 + half] = sums[a * 2 + half] + grads[r - a] * value
            return tuple(sums)

        sums = lax.fori_loop(0, 16, tap_sums, tuple(jnp.zeros((8, 128), F32) for _ in range(14)))
        for index, value in enumerate(sums):
            small_in[index, b : b + 1, :] = jnp.sum(value, axis=0, keepdims=True)
    for part in range(8):
        small_in[part, 7:8, :] = jnp.sum(
            bias_sum[:, part * 128 : part * 128 + 128], axis=0, keepdims=True
        )
    for row in range(5):
        total = jnp.sum(vector_sum[row], axis=0, keepdims=True)
        if row == 3:
            total = total * scale_ref[...]
        for half in range(2):
            small_in[14 + half, row : row + 1, :] = total[:, half * 128 : half * 128 + 128]
    small_copies = [small(small_in, small_core, sibling)]

    finish(big_copies)

    def add_a(index, carry):
        total = sum_core[place_a * 32 + index].astype(F32)
        for step in range(3):
            total = total + from_a[step, index].astype(F32)
        sum_a[index] = total.astype(BF16)
        return carry

    lax.fori_loop(0, 32, add_a, 0, unroll=8)
    big_copies = []
    for step in range(1, 4):
        chunk = lax.rem(place_b + step, 4)
        big_copies.append(big(sum_a.at[pl.ds(chunk * 8, 8)], from_b.at[step - 1], b_peer(step)))

    def own_shift_g(row, carry):
        shift_row(shifted_g, 3 + row)
        return carry

    lax.fori_loop(0, ROWS, own_shift_g, 0)
    finish(small_copies)
    small_sum[...] = small_in[...] + small_core[...]
    small_copies = []
    for step in range(1, 4):
        chunk = lax.rem(x + step, 4)
        small_copies.append(
            small(small_sum.at[pl.ds(chunk * 4, 4)], small_x.at[step - 1], x_peer(step))
        )
    finish(big_copies)

    def add_b(index, carry):
        total = sum_a[place_b * 8 + index].astype(F32)
        for step in range(3):
            total = total + from_b[step, index].astype(F32)
        sum_b[index] = total.astype(BF16)
        return carry

    lax.fori_loop(0, 8, add_b, 0, unroll=8)
    big_copies = []
    for step in range(1, 8):
        big_copies.append(big(sum_b.at[lax.rem(z + step, 8)], from_z.at[step - 1], z_peer(step)))

    def own_conv_g(chunk, carry):
        conv_chunk(shifted_g, taps, True, conv, chunk, OWN_PAIRS, edge_zero)
        return carry

    lax.fori_loop(0, 8, own_conv_g, 0)

    finish(small_copies)
    small_sum_x[...] = small_sum[pl.ds(x * 4, 4)] + small_x[0] + small_x[1] + small_x[2]
    small_copies = []
    for step in range(1, 4):
        chunk = lax.rem(y + step, 4)
        small_copies.append(small(small_sum_x.at[chunk], small_y.at[step - 1], y_peer(step)))
    finish(big_copies)
    total = sum_b[z].astype(F32)
    for step in range(7):
        total = total + from_z[step].astype(F32)
    own = place_a * 32 + place_b * 8 + z
    gathered[core, own] = total.astype(BF16)
    big_copies = []
    for step in range(1, 8):
        big_copies.append(big(gathered.at[core, own], gathered.at[core, own], z_peer(step)))

    lax.fori_loop(8, 16, own_conv_g, 0)

    finish(small_copies)
    small_z[z] = small_sum_x[y] + small_y[0] + small_y[1] + small_y[2]
    small_copies = []
    for step in range(1, 8):
        small_copies.append(small(small_z.at[z], small_z.at[z], z_peer(step)))
    finish(big_copies)
    block = pl.ds(place_a * 32 + place_b * 8, 8)
    big_copies = []
    for step in range(1, 4):
        big_copies.append(big(gathered.at[core, block], gathered.at[core, block], b_peer(step)))

    for copy in halo:
        copy.wait()
    take_ghosts(ghosts_g)
    take_rows(above_g, below_g)
    for row in range(3):
        for side_row in (row, 11 + row):
            wide[side_row, 0:8, :] = edge_zero
            wide[side_row, 136:144, :] = edge_zero

    def rim_shift_g(row, carry):
        shift_row(shifted_g, row)
        shift_row(shifted_g, 11 + row)
        return carry

    lax.fori_loop(0, 3, rim_shift_g, 0)
    finish(small_copies)
    total = small_z[0]
    for step in range(1, 8):
        total = total + small_z[step]
    mine = x * 4 + y
    small_out[mine] = total * factor
    small_copies = []
    for step in range(1, 4):
        small_copies.append(small(small_out.at[mine], small_out.at[mine], y_peer(step)))
    finish(big_copies)
    wide_block = pl.ds(place_a * 32, 32)
    big_copies = []
    for step in range(1, 4):
        big_copies.append(
            big(gathered.at[core, wide_block], gathered.at[core, wide_block], a_peer(step))
        )

    def rim_conv_g(chunk, carry):
        conv_chunk(shifted_g, taps, True, conv, chunk, RIM_PAIRS, None)
        return carry

    lax.fori_loop(0, 16, rim_conv_g, 0)
    for side in range(2):
        partner_side = edge_ref[face * 6 + side * 3 + 1]
        reverse = edge_ref[face * 6 + side * 3 + 2]
        totals = [jnp.zeros((8, CH), F32) for _ in range(3)]
        for a in range(7):
            weights = []
            for offset in range(1, 4):
                weights.append(
                    pick(
                        partner_side,
                        pick(reverse, taps[(6 - a) * 7 + 3 + offset], taps[a * 7 + 3 + offset]),
                        pick(reverse, taps[(6 - a) * 7 + 3 - offset], taps[a * 7 + 3 - offset]),
                    )
                )
            for other in range(3):
                value = ghost_f[side, other, 11 - a : 19 - a, :]
                for depth in range(3 - other):
                    totals[depth] = totals[depth] + weights[depth + other] * value
        for depth in range(3):
            strip_f[side, 0, depth] = totals[depth]
            col = depth if side == 0 else COLS - 1 - depth
            for row in range(ROWS):
                conv[row, col : col + 1, :] = (
                    conv[row, col : col + 1, :] + strip_f[side, 0, depth, row : row + 1, :]
                )
    finish(small_copies)
    mine_x = pl.ds(x * 4, 4)
    small_copies = []
    for step in range(1, 4):
        small_copies.append(small(small_out.at[mine_x], small_out.at[mine_x], x_peer(step)))

    def fields_row(row, carry):
        gfields_ref[row] = (conv[row] + cot_ref[row].astype(F32)).astype(BF16)
        return carry

    lax.fori_loop(0, ROWS, fields_row, 0)
    finish(big_copies)
    big_copies = [big(gathered.at[core], gathered.at[core], sibling)]
    finish(small_copies)
    for a in range(7):
        for half in range(2):
            gkernel_ref[a, :, half * 128 : half * 128 + 128] = small_out[2 * a + half, 0:7, :]
    for part in range(8):
        gbias_ref[part : part + 1, :] = small_out[part, 7:8, :]
    for half in range(2):
        gvectors_ref[:, half * 128 : half * 128 + 128] = small_out[14 + half, 0:5, :]
    finish(big_copies)

    def empty_expand(row, carry):
        rows = pl.ds(pl.multiple_of(row * 16, 16), 16)
        for col in range(8):
            gexpand_ref[rows, col * 128 : col * 128 + 128] = (
                gathered[0, row * 8 + col].astype(F32) * factor
            )
        return carry

    def empty_reduce(row, carry):
        rows = pl.ds(pl.multiple_of(row * 16, 16), 16)
        for col in range(2):
            greduce_ref[rows, col * 128 : col * 128 + 128] = (
                gathered[1, row * 2 + col].astype(F32) * factor
            )
        return carry

    lax.fori_loop(0, 16, empty_expand, 0)
    lax.fori_loop(0, 64, empty_reduce, 0, unroll=4)


def shards(
    fields,
    cotangent,
    edge_match,
    depth_kernel,
    depth_bias,
    norm_gain,
    norm_bias,
    expand_weight,
    expand_bias,
    reduce_weight,
    reduce_bias,
    layer_scale,
):
    vmem = pl.BlockSpec(memory_space=pltpu.VMEM)
    smem = pl.BlockSpec(memory_space=pltpu.SMEM)
    tile = (16, 128)
    cells = ROWS * COLS
    factor = 1.0 / math.sqrt(FACES * TILES * cells)
    halo_scratch = [
        pltpu.VMEM((2, 2, 3, 8, CH), BF16),
        pltpu.VMEM((3, COLS, CH), BF16),
        pltpu.VMEM((3, COLS, CH), BF16),
        pltpu.VMEM((2, 2, 3, 3, 8, CH), BF16),
    ]
    result, gfields, gkernel, gexpand, greduce, gbias, gvectors = pl.pallas_call(
        functools.partial(block_kernel, factor=factor),
        out_shape=(
            jax.ShapeDtypeStruct((ROWS, COLS, CH), BF16),
            jax.ShapeDtypeStruct((ROWS, COLS, CH), BF16),
            jax.ShapeDtypeStruct((7, 7, CH), F32),
            jax.ShapeDtypeStruct((CH, HID), F32),
            jax.ShapeDtypeStruct((HID, CH), F32),
            jax.ShapeDtypeStruct((8, 128), F32),
            jax.ShapeDtypeStruct((5, CH), F32),
        ),
        in_specs=[smem] + [vmem] * 11,
        out_specs=(vmem,) * 7,
        scratch_shapes=[
            pltpu.VMEM((49, 8, CH), F32),
            pltpu.VMEM((14, 144, CH), F32),
            pltpu.VMEM((7, 14, COLS, CH), F32),
            pltpu.VMEM((7, 14, COLS, CH), F32),
            pltpu.VMEM((2, 2, 3, 8, CH), F32),
            *halo_scratch,
            pltpu.VMEM((2, 3, 24, CH), F32),
            pltpu.VMEM((ROWS, COLS, CH), BF16),
            *halo_scratch,
            pltpu.VMEM((ROWS, COLS, CH), F32),
            pltpu.VMEM((ROWS, COLS, CH), F32),
            pltpu.VMEM((ROWS, COLS, 1), F32),
            pltpu.VMEM((cells, CH), BF16),
            pltpu.VMEM((CH, cells), BF16),
            pltpu.VMEM((CH, cells), BF16),
            pltpu.VMEM((cells, HID), F32),
            pltpu.VMEM((cells, HID), BF16),
            pltpu.VMEM((cells, HID), BF16),
            pltpu.VMEM((8, HID), F32),
            pltpu.VMEM((5, 8, CH), F32),
            pltpu.VMEM((2, 128) + tile, BF16),
            pltpu.VMEM((128,) + tile, BF16),
            pltpu.VMEM((128,) + tile, BF16),
            pltpu.VMEM((3, 32) + tile, BF16),
            pltpu.VMEM((32,) + tile, BF16),
            pltpu.VMEM((3, 8) + tile, BF16),
            pltpu.VMEM((8,) + tile, BF16),
            pltpu.VMEM((7,) + tile, BF16),
            pltpu.VMEM((2, 128) + tile, BF16),
            pltpu.VMEM((16, 8, 128), F32),
            pltpu.VMEM((16, 8, 128), F32),
            pltpu.VMEM((16, 8, 128), F32),
            pltpu.VMEM((3, 4, 8, 128), F32),
            pltpu.VMEM((4, 8, 128), F32),
            pltpu.VMEM((3, 8, 128), F32),
            pltpu.VMEM((8, 8, 128), F32),
            pltpu.VMEM((16, 8, 128), F32),
            pltpu.SemaphoreType.DMA((14,)),
            pltpu.SemaphoreType.DMA((14,)),
            pltpu.SemaphoreType.DMA((14,)),
            pltpu.SemaphoreType.DMA((14,)),
            pltpu.SemaphoreType.DMA((28,)),
            pltpu.SemaphoreType.DMA((28,)),
            pltpu.SemaphoreType.DMA((20,)),
            pltpu.SemaphoreType.DMA((20,)),
        ],
        compiler_params=pltpu.CompilerParams(
            collective_id=0, has_side_effects=True, vmem_limit_bytes=62 * 1024 * 1024
        ),
    )(
        edge_match.reshape(-1),
        fields[0],
        cotangent[0],
        depth_kernel,
        depth_bias.reshape(1, CH),
        norm_gain.reshape(1, CH),
        norm_bias.reshape(1, CH),
        expand_weight,
        expand_bias.reshape(1, HID),
        reduce_weight,
        reduce_bias.reshape(1, CH),
        layer_scale.reshape(1, CH),
    )
    return (result[None], gfields[None], gkernel, gexpand, greduce, gbias.reshape(HID), gvectors)


def solution(mesh):
    return jax.shard_map(
        shards,
        mesh=mesh,
        in_specs=(P("face", "tile", None, None),) * 2 + (P(),) * 10,
        out_specs=(P("face", "tile", None, None),) * 2 + (P(),) * 5,
        check_vma=False,
    )
```

time: 157 us -> 85.2 us (0.54)
  other arithmetic: 38.2 us -> 0 us
  matrix products: 14.4 us -> 0 us
  local copies, waits for them, and re-layouts: 17.4 us -> 8.71 us
  between operations: 6.06 us -> 0.67 us
  Pallas kernels: 80.5 us -> 75.5 us
    reduce_sum x7 -> x0, other arithmetic: 21.8 us -> none  [the longest x3 10.3 us: shards(): jnp.sum(grad_conv * padded[row_off:row_off + row_count, col_off:col_off +...]
    dot_general x6 -> x0, matrix products: 14.4 us -> none  [the longest x2 5.24 us: contract_rows(): lax.dot_general(left_side, right_side, (((0,), (0,)), ((), ())), preferre...]
    add x7 -> x0, other arithmetic: 9.44 us -> none  [the longest x1 9.25 us: shards(): interior + kernel[row_off, col_off] * tall[6 - row_off:6 - row_off + row_...]
    slice x24 -> x0, local copies, waits for them, and re-layouts: 5.55 us -> none  [the longest x2 1.46 us: shards(): small[53 * 256:58 * 256].reshape(5, 256)]
    pallas_call x3 -> x1, Pallas kernels: 80.5 us -> 75.5 us  [shards(): pl.pallas_call(functools.partial(block_kernel, factor=factor), out_shape=...]
    select_n x7 -> x0, other arithmetic: 2.79 us -> none  [the longest x1 1.39 us: unpack(): below = jnp.where(last, jnp.zeros_like(below), below)]
    concatenate x2 -> x0, other arithmetic: 2.35 us -> none  [the longest x1 1.72 us: shards(): jnp.concatenate([above.astype(F32), grad_conv, below.astype(F32)], axis=0)]
    squeeze x6 -> x0, local copies, waits for them, and re-layouts: 1.96 us -> none  [the longest x2 1.92 us: unpack(): turned = jnp.flip(ghosts[:, 1], 3)]
where the time goes in v2:
time: 85.2 us; the launch traced here: 84.9 us
  Pallas kernels  75.5 us (89%)
  local copies, waits for them, and re-layouts  8.71 us (10%)
    pallas_call x1, Pallas kernels, shards(): pl.pallas_call(functools.partial(block_kernel, factor=factor), out_shape=...  75.5 us
    unnamed x22, local copies, waits for them, and re-layouts  8.1 us

profile of v2, /device:TPU:1, one launch (start us, length us, event | category | flops | bytes accessed | tf_op | source)
XLA Modules:
  0.0 84.9 jit_solution(11375955426493905935)
XLA Ops:
  0.6 0.0 copy-start.6
  0.6 0.7 copy-done.6
  1.3 0.1 copy.20
  1.4 0.6 reshape.38.edge_ref
  2.0 75.5 %shard_map.171 = (bf16[8,128,256]{2,1,0:T(8,128)(2,1)}, bf16[8,128,256]{2,1,0:T(8,128)(2,1)}, f32[7,7,256]{2,1,0:T(8,128)}, f32[256,1024]{1,0:T(8,128)}, f32[102...) custom-call(s32[48]{0:T(128)} %reshape.38.edge_ref, bf16[8,128,256]{2,1,0:T(8,128)(2,1)} %bitcast.11, ...), custom_call_target="tpu_custom_call" | custom-call | tf_op jit(solution)/shard_map/pallas_call | solution.py:704
  77.5 0.0 copy-start.2
  77.5 0.0 copy-start.1
  77.5 2.0 %copy.28 = bf16[1,8,128,256]{3,2,1,0:T(8,128)(2,1)} copy(bf16[1,8,128,256]{3,2,1,0:T(8,128)(2,1)} %bitcast.14) | data formatting | bytes 1048576
  79.5 0.0 copy-done.2
  79.5 0.0 copy-start.3
  79.5 0.8 copy.29
  80.3 0.0 copy-done.3
  80.4 0.6 copy.30
  81.0 0.0 copy-done.1
  81.0 0.0 copy-start
  81.0 1.0 %copy.31 = f32[256,1024]{1,0:T(8,128)} copy(f32[256,1024]{1,0:T(8,128)S(1)} %copy-done.1) | data formatting | bytes 2097152
  82.0 0.6 copy-done
  82.6 0.0 copy-start.5
  82.6 1.0 %copy.32 = f32[1024,256]{1,0:T(8,128)} copy(f32[1024,256]{1,0:T(8,128)S(1)} %copy-done) | data formatting | bytes 2097152
  83.6 0.0 copy-done.5
  83.6 0.0 copy-start.4
  83.6 0.6 copy.33
  84.2 0.1 copy-done.4
  84.3 0.6 copy.34
Async XLA Ops:
  0.6 0.7 copy-start.6
  77.5 2.0 %copy-start.2 = (bf16[8,128,256]{2,1,0:T(8,128)(2,1)S(1)}, bf16[8,128,256]{2,1,0:T(8,128)(2,1)}, u32[]{:S(2)}) copy-start(bf16[8,128,256]{2,1,0:T(8,128)(2,1)} %get-tuple-element.15) | copy-start | bytes 1572868
  77.5 3.5 %copy-start.1 = (f32[256,1024]{1,0:T(8,128)S(1)}, f32[256,1024]{1,0:T(8,128)}, u32[]{:S(2)}) copy-start(f32[256,1024]{1,0:T(8,128)} %get-tuple-element.31) | copy-start | bytes 3145732
  79.5 0.8 copy-start.3
  81.0 1.6 %copy-start = (f32[1024,256]{1,0:T(8,128)S(1)}, f32[1024,256]{1,0:T(8,128)}, u32[]{:S(2)}) copy-start(f32[1024,256]{1,0:T(8,128)} %get-tuple-element.32) | copy-start | bytes 3145732
  82.6 1.0 %copy-start.5 = (f32[8,128]{1,0:T(8,128)S(1)}, f32[8,128]{1,0:T(8,128)}, u32[]{:S(2)}) copy-start(f32[8,128]{1,0:T(8,128)} %get-tuple-element.19) | copy-start | bytes 12292
  83.6 0.7 copy-start.4

commit v3 on v2

v3 whole, which is shorter than its diff:
```python
import functools
import math

import jax
import jax.numpy as jnp
from jax import lax
from jax.experimental import pallas as pl
from jax.experimental.pallas import tpu as pltpu
from jax.sharding import PartitionSpec as P

EPSILON = 1e-06
ROOT_COEF = 0.7978845608028654
CUBIC_COEF = 0.044715
MESH = pl.DeviceIdType.MESH
FACES = 8
TILES = 32
ROWS = 8
COLS = 128
CH = 256
HID = 1024
F32 = jnp.float32
BF16 = jnp.bfloat16
OWN_PAIRS = [(i, a) for i in range(ROWS) for a in range(7) if 3 <= i + a <= 10]
RIM_PAIRS = [(i, a) for i in range(ROWS) for a in range(7) if not 3 <= i + a <= 10]


def halo_plan(face, tile):
    beside = face + 1 - 2 * lax.rem(face, 2)
    across = lax.rem(face + 4, FACES)
    plan = [
        ("up", (face, lax.rem(tile + TILES - 1, TILES))),
        ("down", (face, lax.rem(tile + 1, TILES))),
    ]
    for link, partner in enumerate((beside, across)):
        for flip in range(2):
            for place in range(3):
                if flip == 0:
                    target = tile + TILES + 1 - place
                else:
                    target = 2 * TILES - tile - place
                plan.append(((link, flip, place), (partner, lax.rem(target, TILES))))
    return plan


def device_at(x, y, z, core):
    return (2 * y + lax.rem(x, 2), 16 * lax.div(x, 2) + 2 * z + core)


class Schedule:
    def __init__(self):
        self.now = 0.0
        self.flows = []

    def add(self, steps, delays):
        self.flows.append([self.now, list(steps), list(delays)])
        self.tick(0.0)

    def step(self, flow):
        flow[1].pop(0)()
        self.now += 0.3
        if flow[1]:
            flow[0] = self.now + flow[2].pop(0)
        else:
            self.flows.remove(flow)

    def tick(self, cost):
        self.now += 1.25 * cost
        while self.flows:
            flow = min(self.flows, key=lambda item: item[0])
            if flow[0] > self.now:
                break
            self.step(flow)

    def drain(self):
        while self.flows:
            flow = min(self.flows, key=lambda item: item[0])
            self.now = max(self.now, flow[0])
            self.step(flow)


def pick(flag, if_one, if_zero):
    return jnp.where(jnp.broadcast_to(flag, if_one.shape) == 1, if_one, if_zero)


def dot_nn(left, right):
    return lax.dot_general(left, right, (((1,), (0,)), ((), ())), preferred_element_type=F32)


def dot_nt(left, right):
    return lax.dot_general(left, right, (((1,), (1,)), ((), ())), preferred_element_type=F32)


def fold(block):
    return jnp.sum(block.reshape(16, 8, block.shape[1]), axis=0)


def conv_chunk(shifted, taps, flipped, out, chunk, pairs, start):
    cols = pl.ds(pl.multiple_of(chunk * 8, 8), 8)
    for half in range(2):
        lanes = slice(half * 128, half * 128 + 128)
        acc = {}
        for i in sorted({i for i, _ in pairs}):
            acc[i] = out[i, cols, lanes] if start is None else start[:, lanes]
        for b in range(7):
            rows = {r: shifted[b, r, cols, lanes] for r in sorted({i + a for i, a in pairs})}
            for a in sorted({a for _, a in pairs}):
                tap = taps[48 - a * 7 - b if flipped else a * 7 + b, :, lanes]
                for i in sorted({i for i, a2 in pairs if a2 == a}):
                    acc[i] = acc[i] + tap * rows[i + a]
        for i, value in acc.items():
            out[i, cols, lanes] = value


def block_kernel(
    edge_ref,
    fields_ref,
    cot_ref,
    taps_ref,
    depth_bias_ref,
    gain_ref,
    norm_bias_ref,
    w1_ref,
    b1_ref,
    w2_ref,
    b2_ref,
    scale_ref,
    result_ref,
    gfields_ref,
    gkernel_ref,
    gexpand_ref,
    greduce_ref,
    gbias_ref,
    gvectors_ref,
    taps,
    wide,
    shifted,
    shifted_g,
    strip_f,
    strips,
    above,
    below,
    ghosts,
    ghost_f,
    rows_g,
    strips_g,
    above_g,
    below_g,
    ghosts_g,
    conv,
    standard,
    inverse,
    normed,
    normed_t,
    cot_branch_t,
    grad_hidden,
    active,
    grad_pre,
    bias_sum,
    vector_sum,
    src,
    from_core,
    sum_core,
    from_plane,
    sum_z,
    gathered,
    small_in,
    small_plane,
    small_line,
    small_out,
    late_in,
    late_line,
    late_plane,
    halo_send,
    halo_recv,
    grad_send,
    grad_recv,
    big_send,
    big_recv,
    small_send,
    small_recv,
    factor,
):
    face, tile = lax.axis_index("face"), lax.axis_index("tile")
    core = lax.rem(tile, 2)
    z = lax.rem(lax.div(tile, 2), 8)
    x = 2 * lax.div(tile, 16) + lax.rem(face, 2)
    y = lax.div(face, 2)
    sibling = device_at(x, y, z, 1 - core)

    mine = 4 * x + y
    lane = 2 * z + core

    def plane_place(step):
        return lax.rem(x + step // 4, 4), lax.rem(y + step % 4, 4)

    def plane_peer(step):
        new_x, new_y = plane_place(step)
        return device_at(new_x, new_y, z, core)

    def z_peer(step):
        return device_at(x, y, lax.rem(z + step, 8), core)

    def line_peer(step):
        new = lax.rem(lane + step, 16)
        return device_at(x, y, lax.div(new, 2), lax.rem(new, 2))

    plan = halo_plan(face, tile)
    barrier = pltpu.get_barrier_semaphore()
    peers = [target for _, target in plan]
    peers += [plane_peer(step) for step in range(1, 16)]
    peers += [line_peer(step) for step in range(1, 16)]
    for peer in peers:
        pl.semaphore_signal(barrier, inc=1, device_id=peer, device_id_type=MESH)

    first = jnp.where(tile == 0, 1, 0)
    last = jnp.where(tile == TILES - 1, 1, 0)
    beside = face + 1 - 2 * lax.rem(face, 2)
    beside_side = jnp.where(edge_ref[0, 0, face] == beside, 0, 1)

    def make_strips(target):
        for row in range(ROWS):
            for depth in range(3):
                for side, col in ((0, 8 + depth), (1, 135 - depth)):
                    piece = wide[3 + row, col : col + 1, :]
                    strip_f[side, 0, depth, row : row + 1, :] = piece
                    strip_f[side, 1, depth, 7 - row : 8 - row, :] = piece
        for flip in range(2):
            for depth in range(3):
                west, east = strip_f[0, flip, depth], strip_f[1, flip, depth]
                target[0, flip, depth] = pick(beside_side, east, west).astype(BF16)
                target[1, flip, depth] = pick(beside_side, west, east).astype(BF16)

    def start_halo(rows, strip, to_above, to_below, to_ghosts, send, recv):
        copies = []
        for index, (kind, target) in enumerate(plan):
            if kind == "up":
                source, landing = rows.at[0:3], to_below
            elif kind == "down":
                source, landing = rows.at[ROWS - 3 : ROWS], to_above
            else:
                link, flip, place = kind
                source, landing = strip.at[link, flip], to_ghosts.at[link, flip, place]
            copy = pltpu.make_async_remote_copy(
                source, landing, send.at[index], recv.at[index], target, MESH
            )
            copy.start()
            copies.append(copy)
        return copies

    def take_ghosts(source):
        for side in range(2):
            reverse = edge_ref[2, side, face]
            other = beside_side if side == 0 else 1 - beside_side
            for place in range(3):
                for depth in range(3):
                    values = [
                        pick(
                            other,
                            source[1, flip, place, depth].astype(F32),
                            source[0, flip, place, depth].astype(F32),
                        )
                        for flip in range(2)
                    ]
                    value = pick(reverse, values[1], values[0])
                    if place == 0:
                        value = pick(first, jnp.zeros_like(value), value)
                    if place == 2:
                        value = pick(last, jnp.zeros_like(value), value)
                    ghost_f[side, depth, place * 8 : place * 8 + 8, :] = value

    def take_rows(source_above, source_below):
        for row in range(3):
            value = source_above[row].astype(F32)
            wide[row, 8:136, :] = pick(first, jnp.zeros_like(value), value)
            value = source_below[row].astype(F32)
            wide[11 + row, 8:136, :] = pick(last, jnp.zeros_like(value), value)

    def shift_row(target, row):
        for b in range(7):
            target[b, row] = wide[row, 5 + b : 133 + b, :]

    for a in range(7):
        block = taps_ref[a].astype(F32)
        for b in range(7):
            taps[a * 7 + b] = jnp.broadcast_to(block[b : b + 1, :], (8, CH))
    edge_zero = jnp.zeros((8, CH), F32)

    def load_row(row, carry):
        wide[3 + row, 0:8, :] = edge_zero
        wide[3 + row, 136:144, :] = edge_zero
        wide[3 + row, 8:136, :] = fields_ref[row].astype(F32)
        return carry

    lax.fori_loop(0, ROWS, load_row, 0)
    make_strips(strips)
    vector_sum[...] = jnp.zeros_like(vector_sum)

    def own_shift(row, carry):
        shift_row(shifted, 3 + row)
        return carry

    lax.fori_loop(0, ROWS, own_shift, 0)
    def cot_row(row, carry):
        cells = pl.ds(pl.multiple_of(row * COLS, COLS), COLS)
        upstream = cot_ref[row].astype(F32)
        scaled = upstream * scale_ref[...]
        half_grad = (0.5 * scaled).astype(BF16)
        cot_branch_t[:, cells] = jnp.transpose(scaled).astype(BF16)
        vector_sum[3] = vector_sum[3] + fold(upstream)
        for part in range(4):
            hidden = slice(part * 256, part * 256 + 256)
            grad_hidden[cells, hidden] = dot_nt(half_grad, w2_ref[hidden, :])
        return carry

    lax.fori_loop(0, ROWS, cot_row, 0)
    pl.semaphore_wait(barrier, len(peers))
    halo = start_halo(fields_ref, strips, above, below, ghosts, halo_send, halo_recv)

    start = jnp.broadcast_to(depth_bias_ref[...], (8, CH))

    def own_conv(chunk, carry):
        conv_chunk(shifted, taps, False, conv, chunk, OWN_PAIRS, start)
        return carry

    lax.fori_loop(1, 15, own_conv, 0)

    halo[0].wait()
    halo[1].wait()
    take_rows(above, below)

    def rim_shift(row, carry):
        shift_row(shifted, row)
        shift_row(shifted, 11 + row)
        return carry

    lax.fori_loop(0, 3, rim_shift, 0)

    def rim_conv(chunk, carry):
        conv_chunk(shifted, taps, False, conv, chunk, RIM_PAIRS, None)
        return carry

    lax.fori_loop(1, 15, rim_conv, 0)
    for copy in halo[2:]:
        copy.wait()
    take_ghosts(ghosts)
    for row in range(14):
        for depth in range(3):
            wide[row, 7 - depth : 8 - depth, :] = ghost_f[0, depth, row + 5 : row + 6, :]
            wide[row, 136 + depth : 137 + depth, :] = ghost_f[1, depth, row + 5 : row + 6, :]

    def edge_shift(row, carry):
        for b in range(7):
            shifted[b, row, 0:8, :] = wide[row, 5 + b : 13 + b, :]
            shifted[b, row, 120:128, :] = wide[row, 125 + b : 133 + b, :]
        return carry

    lax.fori_loop(0, 14, edge_shift, 0)

    def edge_conv(index, carry):
        conv_chunk(shifted, taps, False, conv, index * 15, OWN_PAIRS + RIM_PAIRS, start)
        return carry

    lax.fori_loop(0, 2, edge_conv, 0)

    normed_t[256:272, :] = jnp.ones((16, ROWS * COLS), BF16)

    def norm_row(row, carry):
        cells = pl.ds(pl.multiple_of(row * COLS, COLS), COLS)
        value = conv[row]
        centred = value - jnp.sum(value, axis=1, keepdims=True) * (1.0 / CH)
        variance = jnp.sum(centred * centred, axis=1, keepdims=True) * (1.0 / CH)
        inv = lax.rsqrt(variance + EPSILON)
        std = centred * inv
        standard[row] = std
        inverse[row] = inv
        scaled = std * gain_ref[...] + norm_bias_ref[...]
        normed[cells, :] = (0.5 * scaled).astype(BF16)
        normed_t[0:256, cells] = jnp.transpose(scaled).astype(BF16)
        return carry

    lax.fori_loop(0, ROWS, norm_row, 0)

    schedule = Schedule()

    def part_flow(part):
        counter = [part * 5]
        def send(source, landing, target):
            pltpu.make_async_remote_copy(
                source,
                landing,
                big_send.at[counter[0]],
                big_recv.at[counter[0]],
                target,
                MESH,
            ).start()

        def arrived(like):
            every = pltpu.make_async_remote_copy(
                like, like, big_send.at[counter[0]], big_recv.at[counter[0]], sibling, MESH
            )
            every.wait_send()
            every.wait_recv()
            counter[0] += 1

        def to_core():
            send(src.at[part, 1 - core], from_core.at[part], sibling)

        def to_plane():
            arrived(from_core.at[part])

            def add(index, carry):
                sum_core[part, index] = (
                    src[part, core, index].astype(F32) + from_core[part, index].astype(F32)
                ).astype(BF16)
                return carry

            lax.fori_loop(0, 32, add, 0, unroll=8)
            for step in range(1, 16):
                new_x, new_y = plane_place(step)
                block = sum_core.at[part, pl.ds(8 * new_x + 2 * new_y, 2)]
                send(block, from_plane.at[part, step - 1], plane_peer(step))

        def to_z():
            arrived(from_plane.at[part])
            for index in range(2):
                total = sum_core[part, 2 * mine + index].astype(F32)
                for step in range(15):
                    total = total + from_plane[part, step, index].astype(F32)
                sum_z[part, z, index] = total.astype(BF16)
            for step in range(1, 8):
                send(sum_z.at[part, z], sum_z.at[part, z], z_peer(step))

        def back_plane():
            arrived(sum_z.at[part, 0:7])
            for index in range(2):
                total = sum_z[part, 0, index].astype(F32)
                for step in range(1, 8):
                    total = total + sum_z[part, step, index].astype(F32)
                gathered[part, core, 2 * mine + index] = total.astype(BF16)
            block = gathered.at[part, core, pl.ds(2 * mine, 2)]
            for step in range(1, 16):
                send(block, block, plane_peer(step))

        def back_core():
            arrived(from_plane.at[part])
            send(gathered.at[part, core], gathered.at[part, core], sibling)

        def unpack():
            arrived(gathered.at[part, core])

            def one(row, carry):
                rows = pl.ds(pl.multiple_of(row * 16, 16), 16)
                down = pl.ds(pl.multiple_of(part * 256 + row * 16, 16), 16)
                for col in range(2):
                    across = slice(part * 256 + col * 128, part * 256 + col * 128 + 128)
                    lanes = slice(col * 128, col * 128 + 128)
                    gexpand_ref[rows, across] = gathered[part, 0, row * 2 + col].astype(F32) * factor
                    greduce_ref[down, lanes] = gathered[part, 1, row * 2 + col].astype(F32) * factor
                return carry

            lax.fori_loop(0, 16, one, 0, unroll=4)

        schedule.add(
            [to_core, to_plane, to_z, back_plane, back_core, unpack],
            [1.7, 5.6, 5.6, 5.6, 1.7],
        )

    for part in range(4):
        hidden = slice(part * 256, part * 256 + 256)

        def hidden_row(row, carry):
            cells = pl.ds(pl.multiple_of(row * 256, 256), 256)
            half = dot_nn(normed[cells, :], w1_ref[:, hidden]) + 0.5 * b1_ref[:, hidden]
            square = half * half
            tanhed = jnp.tanh(
                half * (2.0 * ROOT_COEF + (8.0 * ROOT_COEF * CUBIC_COEF) * square)
            )
            plus = 1.0 + tanhed
            value = half * plus
            active[cells, hidden] = value.astype(BF16)
            twice_slope = plus + (value * (1.0 - tanhed)) * (
                2.0 * ROOT_COEF + (24.0 * ROOT_COEF * CUBIC_COEF) * square
            )
            grad_pre[cells, hidden] = (grad_hidden[cells, hidden] * twice_slope).astype(BF16)
            return carry

        lax.fori_loop(0, 2, hidden_row, 0)
        schedule.tick(0.7)
        lax.fori_loop(2, 4, hidden_row, 0)
        schedule.tick(0.7)
        block = dot_nn(normed_t[...], grad_pre[:, hidden])
        bias_sum[:, hidden] = block[256:264, :]
        block = block[0:256, :].astype(BF16)
        for row in range(16):
            for col in range(2):
                src[part, 0, row * 2 + col] = block[
                    row * 16 : row * 16 + 16, col * 128 : col * 128 + 128
                ]
        schedule.tick(0.3)
        block = jnp.transpose(dot_nn(cot_branch_t[...], active[:, hidden])).astype(BF16)
        for row in range(16):
            for col in range(2):
                src[part, 1, row * 2 + col] = block[
                    row * 16 : row * 16 + 16, col * 128 : col * 128 + 128
                ]
        schedule.tick(0.3)
        part_flow(part)

    def grad_row(pair, carry):
        both = dot_nt(grad_pre[pl.ds(pl.multiple_of(pair * 256, 256), 256), :], w1_ref[...])
        for side in range(2):
            row = pair * 2 + side
            grad_normed = both[side * 128 : side * 128 + 128]
            std = standard[row]
            scaled = grad_normed * gain_ref[...]
            mean = jnp.sum(scaled, axis=1, keepdims=True) * (1.0 / CH)
            slant = jnp.sum(scaled * std, axis=1, keepdims=True) * (1.0 / CH)
            grad = (scaled - mean - std * slant) * inverse[row]
            conv[row] = grad
            wide[3 + row, 0:8, :] = edge_zero
            wide[3 + row, 136:144, :] = edge_zero
            wide[3 + row, 8:136, :] = grad
            rows_g[row] = grad.astype(BF16)
            vector_sum[0] = vector_sum[0] + fold(grad)
            vector_sum[1] = vector_sum[1] + fold(grad_normed * std)
            vector_sum[2] = vector_sum[2] + fold(grad_normed)
        return carry

    lax.fori_loop(0, 2, grad_row, 0)
    schedule.tick(0.9)
    lax.fori_loop(2, 4, grad_row, 0)
    make_strips(strips_g)
    halo = start_halo(rows_g, strips_g, above_g, below_g, ghosts_g, grad_send, grad_recv)
    schedule.tick(1.0)

    small_in[...] = jnp.zeros_like(small_in)
    for b in range(7):

        def tap_sums(chunk, carry):
            cols = pl.ds(pl.multiple_of(chunk * 8, 8), 8)
            sums = list(carry)
            for half in range(2):
                lanes = slice(half * 128, half * 128 + 128)
                grads = [conv[i, cols, lanes] for i in range(ROWS)]
                for r in range(14):
                    value = shifted[b, r, cols, lanes]
                    for a in range(7):
                        if 0 <= r - a < ROWS:
                            sums[a * 2 + half] = sums[a * 2 + half] + grads[r - a] * value
            return tuple(sums)

        sums = lax.fori_loop(0, 16, tap_sums, tuple(jnp.zeros((8, 128), F32) for _ in range(14)))
        for index, value in enumerate(sums):
            small_in[index, b : b + 1, :] = jnp.sum(value, axis=0, keepdims=True)
        schedule.tick(0.85)
    for part in range(8):
        small_in[part, 7:8, :] = bias_sum[0:1, part * 128 : part * 128 + 128]
    for row in range(4):
        total = jnp.sum(vector_sum[row], axis=0, keepdims=True)
        if row == 3:
            total = total * scale_ref[...]
        for half in range(2):
            small_in[14 + half, row : row + 1, :] = total[:, half * 128 : half * 128 + 128]

    def small_flow():
        counter = [0]

        def send(source, landing, target):
            pltpu.make_async_remote_copy(
                source,
                landing,
                small_send.at[counter[0]],
                small_recv.at[counter[0]],
                target,
                MESH,
            ).start()

        def arrived(like):
            every = pltpu.make_async_remote_copy(
                like, like, small_send.at[counter[0]], small_recv.at[counter[0]], sibling, MESH
            )
            every.wait_send()
            every.wait_recv()
            counter[0] += 1

        def to_plane():
            for step in range(1, 16):
                new_x, new_y = plane_place(step)
                send(small_in.at[4 * new_x + new_y], small_plane.at[step - 1], plane_peer(step))

        def to_line():
            arrived(small_plane)
            total = small_in[mine]
            for step in range(15):
                total = total + small_plane[step]
            small_line[lane] = total
            for step in range(1, 16):
                send(small_line.at[lane], small_line.at[lane], line_peer(step))

        def back_plane():
            arrived(small_plane)
            total = small_line[0]
            for step in range(1, 16):
                total = total + small_line[step]
            small_out[mine] = total * factor
            for step in range(1, 16):
                send(small_out.at[mine], small_out.at[mine], plane_peer(step))

        def unpack():
            arrived(small_plane)
            for a in range(7):
                for half in range(2):
                    lanes = slice(half * 128, half * 128 + 128)
                    gkernel_ref[a, :, lanes] = small_out[2 * a + half, 0:7, :]
            for part in range(8):
                gbias_ref[part : part + 1, :] = small_out[part, 7:8, :]
            for half in range(2):
                lanes = slice(half * 128, half * 128 + 128)
                gvectors_ref[0:4, lanes] = small_out[14 + half, 0:4, :]

        schedule.add(
            [to_plane, to_line, back_plane, unpack], [5.0, 5.5, 5.0]
        )

    small_flow()

    def result_row(pair, carry):
        both = dot_nn(active[pl.ds(pl.multiple_of(pair * 256, 256), 256), :], w2_ref[...])
        for side in range(2):
            row = pair * 2 + side
            branch = both[side * 128 : side * 128 + 128] + b2_ref[...]
            result_ref[row] = (fields_ref[row].astype(F32) + scale_ref[...] * branch).astype(BF16)
            vector_sum[4] = vector_sum[4] + fold(cot_ref[row].astype(F32) * branch)
        return carry

    lax.fori_loop(0, 2, result_row, 0)
    schedule.tick(0.6)
    lax.fori_loop(2, 4, result_row, 0)
    schedule.tick(0.6)

    late_in[...] = jnp.zeros_like(late_in)
    total = jnp.sum(vector_sum[4], axis=0, keepdims=True)
    for half in range(2):
        late_in[half, 0:1, :] = total[:, half * 128 : half * 128 + 128]

    def late_flow():
        counter = [3]

        def send(source, landing, target):
            pltpu.make_async_remote_copy(
                source,
                landing,
                small_send.at[counter[0]],
                small_recv.at[counter[0]],
                target,
                MESH,
            ).start()

        def arrived(like):
            every = pltpu.make_async_remote_copy(
                like, like, small_send.at[counter[0]], small_recv.at[counter[0]], sibling, MESH
            )
            every.wait_send()
            every.wait_recv()
            counter[0] += 1

        def to_line():
            late_line[lane] = late_in[...]
            for step in range(1, 16):
                send(late_line.at[lane], late_line.at[lane], line_peer(step))

        def to_plane():
            arrived(late_line.at[0:15])
            total = late_line[0]
            for step in range(1, 16):
                total = total + late_line[step]
            late_plane[mine] = total
            for step in range(1, 16):
                send(late_plane.at[mine], late_plane.at[mine], plane_peer(step))

        def unpack():
            arrived(late_plane.at[0:15])
            total = late_plane[0]
            for step in range(1, 16):
                total = total + late_plane[step]
            for half in range(2):
                lanes = slice(half * 128, half * 128 + 128)
                gvectors_ref[4:5, lanes] = total[half, 0:1, :] * factor

        schedule.add([to_line, to_plane, unpack], [5.5, 5.0])

    late_flow()

    def own_shift_g(row, carry):
        shift_row(shifted_g, 3 + row)
        return carry

    def own_conv_g(chunk, carry):
        conv_chunk(shifted_g, taps, True, conv, chunk, OWN_PAIRS, edge_zero)
        return carry

    lax.fori_loop(0, ROWS, own_shift_g, 0)
    schedule.tick(0.65)
    for quarter in range(4):
        lax.fori_loop(quarter * 4, quarter * 4 + 4, own_conv_g, 0)
        schedule.tick(1.1)
    halo[0].wait()
    halo[1].wait()
    take_rows(above_g, below_g)
    for row in range(3):
        for side_row in (row, 11 + row):
            wide[side_row, 0:8, :] = edge_zero
            wide[side_row, 136:144, :] = edge_zero

    def rim_shift_g(row, carry):
        shift_row(shifted_g, row)
        shift_row(shifted_g, 11 + row)
        return carry

    def rim_conv_g(chunk, carry):
        conv_chunk(shifted_g, taps, True, conv, chunk, RIM_PAIRS, None)
        return carry

    lax.fori_loop(0, 3, rim_shift_g, 0)
    schedule.tick(0.6)
    lax.fori_loop(0, 8, rim_conv_g, 0)
    schedule.tick(0.8)
    lax.fori_loop(8, 16, rim_conv_g, 0)
    schedule.tick(0.8)
    for copy in halo[2:]:
        copy.wait()
    take_ghosts(ghosts_g)
    for side in range(2):
        partner_side = edge_ref[1, side, face]
        reverse = edge_ref[2, side, face]
        totals = [jnp.zeros((8, CH), F32) for _ in range(3)]
        for a in range(7):
            weights = []
            for offset in range(1, 4):
                weights.append(
                    pick(
                        partner_side,
                        pick(reverse, taps[(6 - a) * 7 + 3 + offset], taps[a * 7 + 3 + offset]),
                        pick(reverse, taps[(6 - a) * 7 + 3 - offset], taps[a * 7 + 3 - offset]),
                    )
                )
            for other in range(3):
                value = ghost_f[side, other, 11 - a : 19 - a, :]
                for depth in range(3 - other):
                    totals[depth] = totals[depth] + weights[depth + other] * value
        for depth in range(3):
            strip_f[side, 0, depth] = totals[depth]
            col = depth if side == 0 else COLS - 1 - depth
            for row in range(ROWS):
                conv[row, col : col + 1, :] = (
                    conv[row, col : col + 1, :] + strip_f[side, 0, depth, row : row + 1, :]
                )
    schedule.tick(0.5)

    def fields_row(row, carry):
        gfields_ref[row] = (conv[row] + cot_ref[row].astype(F32)).astype(BF16)
        return carry

    lax.fori_loop(0, ROWS, fields_row, 0)
    schedule.tick(0.2)
    schedule.drain()


def copy_out(*refs):
    count = len(refs) // 2
    sems = refs[-1]
    copies = [
        pltpu.make_async_copy(refs[index], refs[count + index], sems.at[index])
        for index in range(count)
    ]
    for copy in copies:
        copy.start()
    for copy in copies:
        copy.wait()


def shards(
    fields,
    cotangent,
    edge_match,
    depth_kernel,
    depth_bias,
    norm_gain,
    norm_bias,
    expand_weight,
    expand_bias,
    reduce_weight,
    reduce_bias,
    layer_scale,
):
    vmem = pl.BlockSpec(memory_space=pltpu.VMEM)
    smem = pl.BlockSpec(memory_space=pltpu.SMEM)
    tile = (16, 128)
    cells = ROWS * COLS
    factor = 1.0 / math.sqrt(FACES * TILES * cells)
    halo_scratch = [
        pltpu.VMEM((2, 2, 3, 8, CH), BF16),
        pltpu.VMEM((3, COLS, CH), BF16),
        pltpu.VMEM((3, COLS, CH), BF16),
        pltpu.VMEM((2, 2, 3, 3, 8, CH), BF16),
    ]
    outputs = pl.pallas_call(
        functools.partial(block_kernel, factor=factor),
        out_shape=(
            jax.ShapeDtypeStruct((ROWS, COLS, CH), BF16),
            jax.ShapeDtypeStruct((ROWS, COLS, CH), BF16),
            jax.ShapeDtypeStruct((7, 7, CH), F32),
            jax.ShapeDtypeStruct((CH, HID), F32),
            jax.ShapeDtypeStruct((HID, CH), F32),
            jax.ShapeDtypeStruct((8, 128), F32),
            jax.ShapeDtypeStruct((5, CH), F32),
        ),
        in_specs=[smem] + [vmem] * 11,
        out_specs=(vmem,) * 7,
        scratch_shapes=[
            pltpu.VMEM((49, 8, CH), F32),
            pltpu.VMEM((14, 144, CH), F32),
            pltpu.VMEM((7, 14, COLS, CH), F32),
            pltpu.VMEM((7, 14, COLS, CH), F32),
            pltpu.VMEM((2, 2, 3, 8, CH), F32),
            *halo_scratch,
            pltpu.VMEM((2, 3, 24, CH), F32),
            pltpu.VMEM((ROWS, COLS, CH), BF16),
            *halo_scratch,
            pltpu.VMEM((ROWS, COLS, CH), F32),
            pltpu.VMEM((ROWS, COLS, CH), F32),
            pltpu.VMEM((ROWS, COLS, 1), F32),
            pltpu.VMEM((cells, CH), BF16),
            pltpu.VMEM((CH + 16, cells), BF16),
            pltpu.VMEM((CH, cells), BF16),
            pltpu.VMEM((cells, HID), F32),
            pltpu.VMEM((cells, HID), BF16),
            pltpu.VMEM((cells, HID), BF16),
            pltpu.VMEM((8, HID), F32),
            pltpu.VMEM((5, 8, CH), F32),
            pltpu.VMEM((4, 2, 32) + tile, BF16),
            pltpu.VMEM((4, 32) + tile, BF16),
            pltpu.VMEM((4, 32) + tile, BF16),
            pltpu.VMEM((4, 15, 2) + tile, BF16),
            pltpu.VMEM((4, 8, 2) + tile, BF16),
            pltpu.VMEM((4, 2, 32) + tile, BF16),
            pltpu.VMEM((16, 8, 128), F32),
            pltpu.VMEM((15, 8, 128), F32),
            pltpu.VMEM((16, 8, 128), F32),
            pltpu.VMEM((16, 8, 128), F32),
            pltpu.VMEM((2, 8, 128), F32),
            pltpu.VMEM((16, 2, 8, 128), F32),
            pltpu.VMEM((16, 2, 8, 128), F32),
            pltpu.SemaphoreType.DMA((14,)),
            pltpu.SemaphoreType.DMA((14,)),
            pltpu.SemaphoreType.DMA((14,)),
            pltpu.SemaphoreType.DMA((14,)),
            pltpu.SemaphoreType.DMA((20,)),
            pltpu.SemaphoreType.DMA((20,)),
            pltpu.SemaphoreType.DMA((5,)),
            pltpu.SemaphoreType.DMA((5,)),
        ],
        compiler_params=pltpu.CompilerParams(
            collective_id=0, has_side_effects=True, vmem_limit_bytes=54 * 1024 * 1024
        ),
    )(
        edge_match.transpose(2, 1, 0),
        fields[0],
        cotangent[0],
        depth_kernel,
        depth_bias.reshape(1, CH),
        norm_gain.reshape(1, CH),
        norm_bias.reshape(1, CH),
        expand_weight,
        expand_bias.reshape(1, HID),
        reduce_weight,
        reduce_bias.reshape(1, CH),
        layer_scale.reshape(1, CH),
    )
    anywhere = pl.BlockSpec(memory_space=pl.ANY)
    result, gfields, gkernel, gexpand, greduce, gbias, gvectors = pl.pallas_call(
        copy_out,
        out_shape=tuple(jax.ShapeDtypeStruct(item.shape, item.dtype) for item in outputs),
        in_specs=[vmem] * 7,
        out_specs=(anywhere,) * 7,
        scratch_shapes=[pltpu.SemaphoreType.DMA((7,))],
    )(*outputs)
    return (result[None], gfields[None], gkernel, gexpand, greduce, gbias.reshape(HID), gvectors)


def solution(mesh):
    return jax.shard_map(
        shards,
        mesh=mesh,
        in_specs=(P("face", "tile", None, None),) * 2 + (P(),) * 10,
        out_specs=(P("face", "tile", None, None),) * 2 + (P(),) * 5,
        check_vma=False,
    )
```

time: 85.2 us -> 71.2 us (0.84)
  local copies, waits for them, and re-layouts: 8.71 us -> 0 us
  Pallas kernels: 75.5 us -> 70.5 us
    pallas_call x1, Pallas kernels: 75.5 us -> 66.8 us  [shards(): pl.pallas_call(functools.partial(block_kernel, factor=factor), out_shape=...]
    unnamed x22 -> x0, local copies, waits for them, and re-layouts: 8.1 us -> none
    pallas_call x0 -> x1, Pallas kernels: none -> 3.63 us  [shards(): pl.pallas_call(copy_out, out_shape=tuple((jax.ShapeDtypeStruct(item.shape...]
where the time goes in v3:
time: 71.2 us; the launch traced here: 71.1 us
  Pallas kernels  70.5 us (99%)
    pallas_call x1, Pallas kernels, shards(): pl.pallas_call(functools.partial(block_kernel, factor=factor), out_shape=...  66.8 us
    pallas_call x1, Pallas kernels, shards(): pl.pallas_call(copy_out, out_shape=tuple((jax.ShapeDtypeStruct(item.shape...  3.63 us

profile of v3, /device:TPU:1, one launch (start us, length us, event | category | flops | bytes accessed | tf_op | source)
XLA Modules:
  0.0 71.1 jit_solution(9698633255580056945)
XLA Ops:
  0.6 66.8 %shard_map.171 = (bf16[8,128,256]{2,1,0:T(8,128)(2,1)}, bf16[8,128,256]{2,1,0:T(8,128)(2,1)}, f32[7,7,256]{2,1,0:T(8,128)}, f32[256,1024]{1,0:T(8,128)}, f32[102...) custom-call(s32[3,2,8]{2,1,0:T(2,128)} %bitcast.15, bf16[8,128,256]{2,1,0:T(8,128)(2,1)} %bitcast.12, ...), custom_call_target="tpu_custom_call" | custom-call | tf_op jit(solution)/shard_map/pallas_call | solution.py:807
  67.5 3.6 %shard_map.172 = (bf16[8,128,256]{2,1,0:T(8,128)(2,1)}, bf16[8,128,256]{2,1,0:T(8,128)(2,1)}, f32[7,7,256]{2,1,0:T(8,128)}, f32[256,1024]{1,0:T(8,128)}, f32[102...) custom-call(bf16[8,128,256]{2,1,0:T(8,128)(2,1)} %get-tuple-element.21.refs_0_, ...), custom_call_target="tpu_custom_call" | custom-call | tf_op jit(solution)/shard_map/pallas_call | solution.py:881

commit v4 on v3

--- a/solution.py
+++ b/solution.py
@@ -59,7 +59,7 @@
         flow[1].pop(0)()
         self.now += 0.3
         if flow[1]:
-            flow[0] = self.now + flow[2].pop(0)
+            flow[0] = self.now + 2.4 * flow[2].pop(0)
         else:
             self.flows.remove(flow)
 
@@ -167,9 +167,6 @@
     small_plane,
     small_line,
     small_out,
-    late_in,
-    late_line,
-    late_plane,
     halo_send,
     halo_recv,
     grad_send,
@@ -232,7 +229,8 @@
 
     def start_halo(rows, strip, to_above, to_below, to_ghosts, send, recv):
         copies = []
-        for index, (kind, target) in enumerate(plan):
+        for index in sorted(range(14), key=lambda i: (i < 2, i < 14 and i >= 2 and plan[i][0][1] == 0)):
+            kind, target = plan[index]
             if kind == "up":
                 source, landing = rows.at[0:3], to_below
             elif kind == "down":
@@ -244,8 +242,8 @@
                 source, landing, send.at[index], recv.at[index], target, MESH
             )
             copy.start()
-            copies.append(copy)
-        return copies
+            copies.append((index, copy))
+        return [copy for _, copy in sorted(copies, key=lambda item: item[0])]
 
     def take_ghosts(source):
         for side in range(2):
@@ -533,6 +531,20 @@
     halo = start_halo(rows_g, strips_g, above_g, below_g, ghosts_g, grad_send, grad_recv)
     schedule.tick(1.0)
 
+    def result_row(pair, carry):
+        both = dot_nn(active[pl.ds(pl.multiple_of(pair * 256, 256), 256), :], w2_ref[...])
+        for side in range(2):
+            row = pair * 2 + side
+            branch = both[side * 128 : side * 128 + 128] + b2_ref[...]
+            result_ref[row] = (fields_ref[row].astype(F32) + scale_ref[...] * branch).astype(BF16)
+            vector_sum[4] = vector_sum[4] + fold(cot_ref[row].astype(F32) * branch)
+        return carry
+
+    lax.fori_loop(0, 2, result_row, 0)
+    schedule.tick(0.6)
+    lax.fori_loop(2, 4, result_row, 0)
+    schedule.tick(0.6)
+
     small_in[...] = jnp.zeros_like(small_in)
     for b in range(7):
 
@@ -555,7 +567,7 @@
         schedule.tick(0.85)
     for part in range(8):
         small_in[part, 7:8, :] = bias_sum[0:1, part * 128 : part * 128 + 128]
-    for row in range(4):
+    for row in range(5):
         total = jnp.sum(vector_sum[row], axis=0, keepdims=True)
         if row == 3:
             total = total * scale_ref[...]
@@ -616,80 +628,13 @@
                 gbias_ref[part : part + 1, :] = small_out[part, 7:8, :]
             for half in range(2):
                 lanes = slice(half * 128, half * 128 + 128)
-                gvectors_ref[0:4, lanes] = small_out[14 + half, 0:4, :]
+                gvectors_ref[:, lanes] = small_out[14 + half, 0:5, :]
 
         schedule.add(
             [to_plane, to_line, back_plane, unpack], [5.0, 5.5, 5.0]
         )
 
     small_flow()
-
-    def result_row(pair, carry):
-        both = dot_nn(active[pl.ds(pl.multiple_of(pair * 256, 256), 256), :], w2_ref[...])
-        for side in range(2):
-            row = pair * 2 + side
-            branch = both[side * 128 : side * 128 + 128] + b2_ref[...]
-            result_ref[row] = (fields_ref[row].astype(F32) + scale_ref[...] * branch).astype(BF16)
-            vector_sum[4] = vector_sum[4] + fold(cot_ref[row].astype(F32) * branch)
-        return carry
-
-    lax.fori_loop(0, 2, result_row, 0)
-    schedule.tick(0.6)
-    lax.fori_loop(2, 4, result_row, 0)
-    schedule.tick(0.6)
-
-    late_in[...] = jnp.zeros_like(late_in)
-    total = jnp.sum(vector_sum[4], axis=0, keepdims=True)
-    for half in range(2):
-        late_in[half, 0:1, :] = total[:, half * 128 : half * 128 + 128]
-
-    def late_flow():
-        counter = [3]
-
-        def send(source, landing, target):
-            pltpu.make_async_remote_copy(
-                source,
-                landing,
-                small_send.at[counter[0]],
-                small_recv.at[counter[0]],
-                target,
-                MESH,
-            ).start()
-
-        def arrived(like):
-            every = pltpu.make_async_remote_copy(
-                like, like, small_send.at[counter[0]], small_recv.at[counter[0]], sibling, MESH
-            )
-            every.wait_send()
-            every.wait_recv()
-            counter[0] += 1
-
-        def to_line():
-            late_line[lane] = late_in[...]
-            for step in range(1, 16):
-                send(late_line.at[lane], late_line.at[lane], line_peer(step))
-
-        def to_plane():
-            arrived(late_line.at[0:15])
-            total = late_line[0]
-            for step in range(1, 16):
-                total = total + late_line[step]
-            late_plane[mine] = total
-            for step in range(1, 16):
-                send(late_plane.at[mine], late_plane.at[mine], plane_peer(step))
-
-        def unpack():
-            arrived(late_plane.at[0:15])
-            total = late_plane[0]
-            for step in range(1, 16):
-                total = total + late_plane[step]
-            for half in range(2):
-                lanes = slice(half * 128, half * 128 + 128)
-                gvectors_ref[4:5, lanes] = total[half, 0:1, :] * factor
-
-        schedule.add([to_line, to_plane, unpack], [5.5, 5.0])
-
-    late_flow()
 
     def own_shift_g(row, carry):
         shift_row(shifted_g, 3 + row)
@@ -767,15 +712,30 @@
 
 
 def copy_out(*refs):
-    count = len(refs) // 2
-    sems = refs[-1]
-    copies = [
-        pltpu.make_async_copy(refs[index], refs[count + index], sems.at[index])
-        for index in range(count)
-    ]
-    for copy in copies:
+    inputs, outputs, buffers = refs[:7], refs[7:14], refs[14:21]
+    in_sem, out_sem = refs[21:]
+    pieces = []
+    for item in range(7):
+        count = 4 if item in (3, 4) else 1
+        rows = inputs[item].shape[0] // count
+        for part in range(count):
+            pieces.append((item, pl.ds(part * rows, rows)))
+    arrivals = []
+    for index, (item, rows) in enumerate(pieces):
+        copy = pltpu.make_async_copy(
+            inputs[item].at[rows], buffers[item].at[rows], in_sem.at[index]
+        )
         copy.start()
-    for copy in copies:
+        arrivals.append(copy)
+    departures = []
+    for index, (item, rows) in enumerate(pieces):
+        arrivals[index].wait()
+        copy = pltpu.make_async_copy(
+            buffers[item].at[rows], outputs[item].at[rows], out_sem.at[index]
+        )
+        copy.start()
+        departures.append(copy)
+    for copy in departures:
         copy.wait()
 
 
@@ -848,9 +808,6 @@
             pltpu.VMEM((15, 8, 128), F32),
             pltpu.VMEM((16, 8, 128), F32),
             pltpu.VMEM((16, 8, 128), F32),
-            pltpu.VMEM((2, 8, 128), F32),
-            pltpu.VMEM((16, 2, 8, 128), F32),
-            pltpu.VMEM((16, 2, 8, 128), F32),
             pltpu.SemaphoreType.DMA((14,)),
             pltpu.SemaphoreType.DMA((14,)),
             pltpu.SemaphoreType.DMA((14,)),
@@ -881,9 +838,10 @@
     result, gfields, gkernel, gexpand, greduce, gbias, gvectors = pl.pallas_call(
         copy_out,
         out_shape=tuple(jax.ShapeDtypeStruct(item.shape, item.dtype) for item in outputs),
-        in_specs=[vmem] * 7,
+        in_specs=[anywhere] * 7,
         out_specs=(anywhere,) * 7,
-        scratch_shapes=[pltpu.SemaphoreType.DMA((7,))],
+        scratch_shapes=[pltpu.VMEM(item.shape, item.dtype) for item in outputs]
+        + [pltpu.SemaphoreType.DMA((13,)), pltpu.SemaphoreType.DMA((13,))],
     )(*outputs)
     return (result[None], gfields[None], gkernel, gexpand, greduce, gbias.reshape(HID), gvectors)
 

time: 71.2 us -> 64.4 us (0.904)
  Pallas kernels: 70.5 us -> 63.6 us
    pallas_call x1, Pallas kernels: 66.8 us -> 60.7 us  [shards(): pl.pallas_call(functools.partial(block_kernel, factor=factor), out_shape=...]
where the time goes in v4:
time: 64.4 us; the launch traced here: 64.3 us
  Pallas kernels  63.6 us (99%)
  between operations  0.65 us (1%)
    pallas_call x1, Pallas kernels, shards(): pl.pallas_call(functools.partial(block_kernel, factor=factor), out_shape=...  60.7 us
    pallas_call x1, Pallas kernels, shards(): pl.pallas_call(copy_out, out_shape=tuple((jax.ShapeDtypeStruct(item.shape...  2.94 us

profile of v4, /device:TPU:1, one launch (start us, length us, event | category | flops | bytes accessed | tf_op | source)
XLA Modules:
  0.0 64.3 jit_solution(13950433416357377402)
XLA Ops:
  0.6 60.7 %shard_map.171 = (bf16[8,128,256]{2,1,0:T(8,128)(2,1)}, bf16[8,128,256]{2,1,0:T(8,128)(2,1)}, f32[7,7,256]{2,1,0:T(8,128)}, f32[256,1024]{1,0:T(8,128)}, f32[102...) custom-call(s32[3,2,8]{2,1,0:T(2,128)} %bitcast.15, bf16[8,128,256]{2,1,0:T(8,128)(2,1)} %bitcast.12, ...), custom_call_target="tpu_custom_call" | custom-call | tf_op jit(solution)/shard_map/pallas_call | solution.py:767
  61.3 2.9 %shard_map.172 = (bf16[8,128,256]{2,1,0:T(8,128)(2,1)}, bf16[8,128,256]{2,1,0:T(8,128)(2,1)}, f32[7,7,256]{2,1,0:T(8,128)}, f32[256,1024]{1,0:T(8,128)}, f32[102...) custom-call(bf16[8,128,256]{2,1,0:T(8,128)(2,1)} %get-tuple-element.21.refs_0_, ...), custom_call_target="tpu_custom_call" | custom-call | tf_op jit(solution)/shard_map/pallas_call | solution.py:838

commit v5 on v4

--- a/solution.py
+++ b/solution.py
@@ -467,7 +467,7 @@
         hidden = slice(part * 256, part * 256 + 256)
 
         def hidden_row(row, carry):
-            cells = pl.ds(pl.multiple_of(row * 256, 256), 256)
+            cells = pl.ds(pl.multiple_of(row * 512, 512), 512)
             half = dot_nn(normed[cells, :], w1_ref[:, hidden]) + 0.5 * b1_ref[:, hidden]
             square = half * half
             tanhed = jnp.tanh(
@@ -482,9 +482,9 @@
             grad_pre[cells, hidden] = (grad_hidden[cells, hidden] * twice_slope).astype(BF16)
             return carry
 
-        lax.fori_loop(0, 2, hidden_row, 0)
+        lax.fori_loop(0, 1, hidden_row, 0)
         schedule.tick(0.7)
-        lax.fori_loop(2, 4, hidden_row, 0)
+        lax.fori_loop(1, 2, hidden_row, 0)
         schedule.tick(0.7)
         block = dot_nn(normed_t[...], grad_pre[:, hidden])
         bias_sum[:, hidden] = block[256:264, :]

time: 64.4 us -> 62.7 us (0.974)
  Pallas kernels: 63.6 us -> 62 us
    pallas_call x1, Pallas kernels: 60.7 us -> 59 us  [shards(): pl.pallas_call(functools.partial(block_kernel, factor=factor), out_shape=...]
where the time goes in v5:
time: 62.7 us; the launch traced here: 62.6 us
  Pallas kernels  62 us (99%)
  between operations  0.65 us (1%)
    pallas_call x1, Pallas kernels, shards(): pl.pallas_call(functools.partial(block_kernel, factor=factor), out_shape=...  59 us
    pallas_call x1, Pallas kernels, shards(): pl.pallas_call(copy_out, out_shape=tuple((jax.ShapeDtypeStruct(item.shape...  2.94 us

profile of v5, /device:TPU:1, one launch (start us, length us, event | category | flops | bytes accessed | tf_op | source)
XLA Modules:
  0.0 62.6 jit_solution(3486468597596988344)
XLA Ops:
  0.6 59.0 %shard_map.171 = (bf16[8,128,256]{2,1,0:T(8,128)(2,1)}, bf16[8,128,256]{2,1,0:T(8,128)(2,1)}, f32[7,7,256]{2,1,0:T(8,128)}, f32[256,1024]{1,0:T(8,128)}, f32[102...) custom-call(s32[3,2,8]{2,1,0:T(2,128)} %bitcast.15, bf16[8,128,256]{2,1,0:T(8,128)(2,1)} %bitcast.12, ...), custom_call_target="tpu_custom_call" | custom-call | tf_op jit(solution)/shard_map/pallas_call | solution.py:767
  59.7 2.9 %shard_map.172 = (bf16[8,128,256]{2,1,0:T(8,128)(2,1)}, bf16[8,128,256]{2,1,0:T(8,128)(2,1)}, f32[7,7,256]{2,1,0:T(8,128)}, f32[256,1024]{1,0:T(8,128)}, f32[102...) custom-call(bf16[8,128,256]{2,1,0:T(8,128)(2,1)} %get-tuple-element.21.refs_0_, ...), custom_call_target="tpu_custom_call" | custom-call | tf_op jit(solution)/shard_map/pallas_call | solution.py:838
